TPU v7x, 32 devices: a whole 2x2x4 slice. The times are simulated.
32 devices in a mesh: groups: 2 (over x), expert: 16 (over z, y, core).
Axes of the slice: x: 2, y: 2, z: 4, core: 2. Of those that a mesh axis runs over, the one named last changes fastest.
Arguments:
- tokens_in: bfloat16 [4096, 1024], P(('groups', 'expert')), parts along dimension 0, may hold values from -6 to 6
- grad_out: bfloat16 [4096, 1024], P(('groups', 'expert')), parts along dimension 0, may hold values from -6 to 6
- gates: bfloat16 [4096, 8], P(('groups', 'expert')), parts along dimension 0, may hold values from 0.049804688 to 0.5
- expert_ids: int32 [4096, 8], P(('groups', 'expert')), parts along dimension 0, may hold values from 0 to 15, as said below
- replica_table: int32 [32], P('groups'), parts along dimension 0, may hold values from 0 to 15, as said below
- w_gate: bfloat16 [16, 1024, 384], P('expert'), may hold values from -0.1875 to 0.1875
- w_up: bfloat16 [16, 1024, 384], P('expert'), may hold values from -0.1875 to 0.1875
- w_down: bfloat16 [16, 384, 1024], P('expert'), may hold values from -0.3125 to 0.3125
Outputs:
- grad_tokens: bfloat16 [4096, 1024], P(('groups', 'expert')), parts along dimension 0
- grad_gates: bfloat16 [4096, 8], P(('groups', 'expert')), parts along dimension 0
- grad_w_gate: bfloat16 [32, 1024, 384], P(('groups', 'expert')), parts along dimension 0
- grad_w_up: bfloat16 [32, 1024, 384], P(('groups', 'expert')), parts along dimension 0
- grad_w_down: bfloat16 [32, 384, 1024], P(('groups', 'expert')), parts along dimension 0
There are 2 independent parts, one for each index of `groups`. A program takes and returns all parts, laid end to end along the dimension named above; an argument that names none is the same for every part. Nothing has to cross between parts.
Inputs may be any that keep to these rules, and one draw needn't show every extreme that they name: `expert_ids`: each row names 8 different experts. `replica_table`: entry d is the expert whose weights device d holds in its replica slot.
All inputs are finite; a program needn't handle non-finite values.
Results may differ from a plain program's by a relative error of at most 0.0057.
Values may be sent and summed in bfloat16 or wider, within the bound.
A program may use at most 128 MiB of HBM per device.

v0:
```python
import jax
import jax.numpy as jnp
from jax import lax
from jax.sharding import PartitionSpec as P

TOP = 8


contract_rows = (((0,), (0,)), ((), ()))
contract_cols = (((1,), (1,)), ((), ()))


def plan_routes(row_ids, replica_table, source, devices, home_cap, rep_cap):
    flat_ids = row_ids.reshape(-1)
    expert_axis = jnp.arange(devices, dtype=jnp.int32)
    hosted = (replica_table[None, :] == expert_axis[:, None]).astype(jnp.int32)
    copies = 1 + jnp.sum(hosted, axis=1)
    replica_order = jnp.cumsum(hosted, axis=1) - hosted
    chosen = (flat_ids[:, None] == expert_axis[None, :]).astype(jnp.int32)
    row_rank = jnp.sum((jnp.cumsum(chosen, axis=0) - chosen) * chosen, axis=1)
    row_copies = jnp.take(copies, flat_ids, axis=0)
    copy_index = (row_rank + source) % row_copies
    at_home = copy_index == 0
    matched = (jnp.take(hosted, flat_ids, axis=0) == 1) & (
        jnp.take(replica_order, flat_ids, axis=0) == (copy_index - 1)[:, None]
    )
    replica_device = jnp.sum(jnp.where(matched, expert_axis[None, :], 0), axis=1)
    target = jnp.where(at_home, flat_ids, replica_device)
    bucket = target * 2 + jnp.where(at_home, 0, 1)
    bucket_hot = (bucket[:, None] == jnp.arange(2 * devices, dtype=jnp.int32)[None, :]).astype(
        jnp.int32
    )
    position = jnp.sum((jnp.cumsum(bucket_hot, axis=0) - bucket_hot) * bucket_hot, axis=1)
    slot_width = home_cap + rep_cap
    kept_rows = jnp.where(at_home, position < home_cap, position < rep_cap)
    slot_index = target * slot_width + jnp.where(at_home, position, home_cap + position)
    slot_index = jnp.where(kept_rows, slot_index, devices * slot_width)
    return (slot_index, kept_rows)


def expert_grads(rows_x, rows_dy, rows_gate, gate_w, up_w, down_w):
    pre_gate = jnp.dot(rows_x, gate_w, preferred_element_type=jnp.float32)
    pre_up = jnp.dot(rows_x, up_w, preferred_element_type=jnp.float32)
    sigmoid_gate = jax.nn.sigmoid(pre_gate)
    activated = pre_gate * sigmoid_gate
    product = activated * pre_up
    hidden = product.astype(jnp.bfloat16)
    back_hidden = lax.dot_general(
        rows_dy, down_w, contract_cols, preferred_element_type=jnp.float32
    )
    gate_grad = jnp.sum(
        lax.optimization_barrier(hidden).astype(jnp.float32) * back_hidden, axis=1
    ).astype(jnp.bfloat16)
    gate_value = rows_gate.astype(jnp.float32)[:, None]
    weighted = (gate_value * product).astype(jnp.bfloat16)
    down_grad = lax.dot_general(
        weighted, rows_dy, contract_rows, preferred_element_type=jnp.float32
    )
    scaled = gate_value * back_hidden
    grad_pre_gate = (
        scaled * pre_up * sigmoid_gate * (1.0 + pre_gate * (1.0 - sigmoid_gate))
    ).astype(jnp.bfloat16)
    grad_pre_up = (scaled * activated).astype(jnp.bfloat16)
    gate_w_grad = lax.dot_general(
        rows_x, grad_pre_gate, contract_rows, preferred_element_type=jnp.float32
    )
    up_w_grad = lax.dot_general(
        rows_x, grad_pre_up, contract_rows, preferred_element_type=jnp.float32
    )
    input_grad = lax.dot_general(
        grad_pre_gate, gate_w, contract_cols, preferred_element_type=jnp.float32
    )
    input_grad = input_grad + lax.dot_general(
        grad_pre_up, up_w, contract_cols, preferred_element_type=jnp.float32
    )
    return (input_grad.astype(jnp.bfloat16), gate_grad, gate_w_grad, up_w_grad, down_grad)


def on_device(tokens_in, grad_out, gates, expert_ids, replica_table, w_gate, w_up, w_down):
    devices = lax.axis_size("expert")
    source = lax.axis_index("expert")
    tok_rows = tokens_in.shape[0]
    home_cap = max(2, 5 * tok_rows * TOP // (4 * devices))
    rep_cap = max(2, tok_rows * TOP // (2 * devices))
    slot_width = home_cap + rep_cap
    model_width = tokens_in.shape[1]
    hidden_units = w_gate.shape[2]
    zero_bf = jnp.zeros((), jnp.bfloat16)
    slot_index, kept_rows = plan_routes(
        expert_ids, replica_table, source, devices, home_cap, rep_cap
    )
    routed = slot_index.shape[0]
    slot_fill = (
        jnp.full((devices * slot_width + 1,), -1, jnp.int32)
        .at[slot_index]
        .set(jnp.arange(routed, dtype=jnp.int32))[:-1]
    )
    filled = slot_fill >= 0
    clipped = jnp.maximum(slot_fill, 0)
    token_row = clipped // TOP
    top_index = clipped % TOP
    send_x = jnp.where(filled[:, None], jnp.take(tokens_in, token_row, axis=0), zero_bf).reshape(
        devices, slot_width, model_width
    )
    send_dy = jnp.where(filled[:, None], jnp.take(grad_out, token_row, axis=0), zero_bf).reshape(
        devices, slot_width, model_width
    )
    send_gate = jnp.where(filled, gates[token_row, top_index], zero_bf).reshape(devices, slot_width)
    piece_gate = w_gate.reshape(devices, model_width // devices, hidden_units)
    piece_up = w_up.reshape(devices, model_width // devices, hidden_units)
    piece_down = w_down.reshape(devices, hidden_units // devices, model_width)
    recv_x, recv_dy, recv_gate = (
        lax.all_to_all(send_x, "expert", split_axis=0, concat_axis=0, tiled=True),
        lax.all_to_all(send_dy, "expert", split_axis=0, concat_axis=0, tiled=True),
        lax.all_to_all(send_gate, "expert", split_axis=0, concat_axis=0, tiled=True),
    )
    spread_gate, spread_up, spread_down = (
        lax.all_to_all(piece_gate, "expert", split_axis=0, concat_axis=0, tiled=True),
        lax.all_to_all(piece_up, "expert", split_axis=0, concat_axis=0, tiled=True),
        lax.all_to_all(piece_down, "expert", split_axis=0, concat_axis=0, tiled=True),
    )
    copy_gate, copy_up, copy_down = (
        lax.all_to_all(
            jnp.take(spread_gate, replica_table, axis=0),
            "expert",
            split_axis=0,
            concat_axis=0,
            tiled=True,
        ),
        lax.all_to_all(
            jnp.take(spread_up, replica_table, axis=0),
            "expert",
            split_axis=0,
            concat_axis=0,
            tiled=True,
        ),
        lax.all_to_all(
            jnp.take(spread_down, replica_table, axis=0),
            "expert",
            split_axis=0,
            concat_axis=0,
            tiled=True,
        ),
    )
    home_grads = expert_grads(
        recv_x[:, :home_cap].reshape(-1, model_width),
        recv_dy[:, :home_cap].reshape(-1, model_width),
        recv_gate[:, :home_cap].reshape(-1),
        w_gate[0],
        w_up[0],
        w_down[0],
    )
    extra_grads = expert_grads(
        recv_x[:, home_cap:].reshape(-1, model_width),
        recv_dy[:, home_cap:].reshape(-1, model_width),
        recv_gate[:, home_cap:].reshape(-1),
        copy_gate.reshape(model_width, hidden_units),
        copy_up.reshape(model_width, hidden_units),
        copy_down.reshape(hidden_units, model_width),
    )
    back_x = jnp.concatenate(
        [
            home_grads[0].reshape(devices, home_cap, model_width),
            extra_grads[0].reshape(devices, rep_cap, model_width),
        ],
        axis=1,
    )
    back_gate = jnp.concatenate(
        [home_grads[1].reshape(devices, home_cap), extra_grads[1].reshape(devices, rep_cap)], axis=1
    )
    replica_gate = (
        extra_grads[2].astype(jnp.bfloat16).reshape(devices, model_width // devices, hidden_units)
    )
    replica_up = (
        extra_grads[3].astype(jnp.bfloat16).reshape(devices, model_width // devices, hidden_units)
    )
    replica_down = (
        extra_grads[4].astype(jnp.bfloat16).reshape(devices, hidden_units // devices, model_width)
    )
    returned_x, returned_gate, gate_partial_grad, up_partial_grad, down_partial_grad = (
        lax.all_to_all(back_x, "expert", split_axis=0, concat_axis=0, tiled=True),
        lax.all_to_all(back_gate, "expert", split_axis=0, concat_axis=0, tiled=True),
        lax.all_to_all(replica_gate, "expert", split_axis=0, concat_axis=0, tiled=True),
        lax.all_to_all(replica_up, "expert", split_axis=0, concat_axis=0, tiled=True),
        lax.all_to_all(replica_down, "expert", split_axis=0, concat_axis=0, tiled=True),
    )
    owner_device_table = (
        replica_table[None, :] == jnp.arange(devices, dtype=jnp.int32)[:, None]
    ).astype(jnp.bfloat16)
    summed_gate = jnp.einsum(
        "qt,tym->qym", owner_device_table, gate_partial_grad, preferred_element_type=jnp.float32
    ).astype(jnp.bfloat16)
    summed_up = jnp.einsum(
        "qt,tym->qym", owner_device_table, up_partial_grad, preferred_element_type=jnp.float32
    ).astype(jnp.bfloat16)
    summed_down = jnp.einsum(
        "qt,tym->qym", owner_device_table, down_partial_grad, preferred_element_type=jnp.float32
    ).astype(jnp.bfloat16)
    total_gate, total_up, total_down = (
        lax.all_to_all(summed_gate, "expert", split_axis=0, concat_axis=0, tiled=True),
        lax.all_to_all(summed_up, "expert", split_axis=0, concat_axis=0, tiled=True),
        lax.all_to_all(summed_down, "expert", split_axis=0, concat_axis=0, tiled=True),
    )
    grad_w_gate = (
        home_grads[2] + total_gate.reshape(model_width, hidden_units).astype(jnp.float32)
    ).astype(jnp.bfloat16)[None]
    grad_w_up = (
        home_grads[3] + total_up.reshape(model_width, hidden_units).astype(jnp.float32)
    ).astype(jnp.bfloat16)[None]
    grad_w_down = (
        home_grads[4] + total_down.reshape(hidden_units, model_width).astype(jnp.float32)
    ).astype(jnp.bfloat16)[None]
    clipped_slot = jnp.minimum(slot_index, devices * slot_width - 1)
    flat_back = returned_x.reshape(devices * slot_width, model_width)
    gathered_rows = jnp.where(
        kept_rows[:, None],
        jnp.take(flat_back, clipped_slot, axis=0).astype(jnp.float32),
        jnp.float32(0.0),
    )
    grad_tokens = jnp.sum(gathered_rows.reshape(-1, TOP, model_width), axis=1).astype(jnp.bfloat16)
    grad_gates = jnp.where(
        kept_rows, jnp.take(returned_gate.reshape(-1), clipped_slot, axis=0), zero_bf
    ).reshape(-1, TOP)
    return (grad_tokens, grad_gates, grad_w_gate, grad_w_up, grad_w_down)


def solution(mesh):
    return jax.shard_map(
        on_device,
        mesh=mesh,
        in_specs=(
            P(("groups", "expert"), None),
            P(("groups", "expert"), None),
            P(("groups", "expert"), None),
            P(("groups", "expert"), None),
            P("groups"),
            P("expert", None, None),
            P("expert", None, None),
            P("expert", None, None),
        ),
        out_specs=(
            P(("groups", "expert"), None),
            P(("groups", "expert"), None),
            P(("groups", "expert"), None, None),
            P(("groups", "expert"), None, None),
            P(("groups", "expert"), None, None),
        ),
        check_vma=False,
    )
```

profile of v0, /device:TPU:10, one launch (start us, length us, event | category | flops | bytes accessed | tf_op | source)
XLA Modules:
  0.0 643.7 jit_solution(17578999911705583110)
XLA Ops:
  19.8 5.9 broadcast_add_fusion.2
  26.4 9.0 %reduce-window.16 = s32[32,8,128]{2,1,0:T(8,128)S(1)} reduce-window(s32[32,8,128]{2,1,0:T(8,128)S(1)} %fusion.30, s32[]{:T(128)} %constant.107.clone.1), window={size=1x1x128 pad=0_0x0_0x127_0}, to_apply=%region_6.8 | reduce-window | flops 4161536 | bytes 262148 | tf_op jit(solution)/shard_map/reduce-window.2
  40.8 13.4 %gather_fusion = bf16[1792]{0:T(1024)(128)(2,1)S(1)} fusion(bf16[128,8]{0,1:T(8,128)(2,1)S(1)} %copy-done.2, s32[1792]{0:T(1024)S(1)} %get-tuple-element.39), kind=kCustom, calls=%fused_computation.6 | custom fusion | bytes 21504 | tf_op jit(solution)/shard_map/gather | solution.py:108
  54.3 11.1 %all_to_all.93 = bf16[16,1,112]{2,1,0:T(2,128)(2,1)S(1)} all-to-all(bf16[16,1,112]{2,1,0:T(2,128)(2,1)S(1)} %select_n.440), channel_id=1, replica_groups=mesh['groups'=2,'expert'=16] {'expert'}, dimensions={0} | all-to-all | bytes 7168 | tf_op jit(solution)/shard_map/all_to_all | solution.py:115
  65.4 23.6 %all_to_all.94 = bf16[16,64,384]{2,1,0:T(8,128)(2,1)S(1)} all-to-all(bf16[16,64,384]{2,1,0:T(8,128)(2,1)S(1)} %bitcast.164), channel_id=1, replica_groups=mesh['groups'=2,'expert'=16] {'expert'}, dimensions={0} | all-to-all | bytes 1572864 | tf_op jit(solution)/shard_map/all_to_all | solution.py:119
  89.0 23.8 %all_to_all.95 = bf16[16,64,384]{2,1,0:T(8,128)(2,1)S(1)} all-to-all(bf16[16,64,384]{2,1,0:T(8,128)(2,1)S(1)} %bitcast.163), channel_id=1, replica_groups=mesh['groups'=2,'expert'=16] {'expert'}, dimensions={0} | all-to-all | bytes 1572864 | tf_op jit(solution)/shard_map/all_to_all | solution.py:118
  122.7 13.4 %all-to-all-done.3 = bf16[16,24,1024]{2,1,0:T(8,128)(2,1)S(1)} async-done(((bf16[16,24,1024]{2,1,0:T(8,128)(2,1)}), bf16[16,24,1024]{2,1,0:T(8,128)(2,1)S(1)}, u32[]{:S(2)}, u32[]{:S(2)}) %all-to-all-start.3) | async-done | bytes 786464 | tf_op jit(solution)/shard_map/all_to_all | solution.py:120
  136.1 24.5 %all_to_all.96 = bf16[16,64,384]{2,1,0:T(8,128)(2,1)S(1)} all-to-all(bf16[16,64,384]{2,1,0:T(8,128)(2,1)S(1)} %get-tuple-element.55), channel_id=1, replica_groups=mesh['groups'=2,'expert'=16] {'expert'}, dimensions={0} | all-to-all | bytes 1572864 | tf_op jit(solution)/shard_map/all_to_all | solution.py:130
  165.3 6.6 %gather_fusion.7 = bf16[1792,1024]{1,0:T(8,128)(2,1)} fusion(bf16[128,1024]{1,0:T(8,128)(2,1)S(1)} %copy-done, s32[2048]{0:T(1024)S(1)} %pad_clamp_fusion), kind=kCustom, calls=%fused_computation.4.clone | custom fusion | bytes 7347200 | tf_op jit(solution)/shard_map/jit(_take)/gather | solution.py:102
  171.9 6.6 %gather_fusion.6 = bf16[1792,1024]{1,0:T(8,128)(2,1)} fusion(bf16[128,1024]{1,0:T(8,128)(2,1)S(1)} %copy-done.3, s32[2048]{0:T(1024)S(1)} %pad_clamp_fusion), kind=kCustom, calls=%fused_computation.1.clone | custom fusion | bytes 7347200 | tf_op jit(solution)/shard_map/jit(_take)/gather | solution.py:105
  178.5 5.8 select_select_fusion.1
  184.3 87.0 %all_to_all.97 = bf16[16,112,1024]{2,1,0:T(8,128)(2,1)} all-to-all(bf16[16,112,1024]{2,1,0:T(8,128)(2,1)} %bitcast.152), channel_id=1, replica_groups=mesh['groups'=2,'expert'=16] {'expert'}, dimensions={0} | all-to-all | bytes 7340032 | tf_op jit(solution)/shard_map/all_to_all | solution.py:113
  280.4 75.8 %all-to-all-done.1 = bf16[16,112,1024]{2,1,0:T(8,128)(2,1)} async-done(((bf16[16,112,1024]{2,1,0:T(8,128)(2,1)}), bf16[16,112,1024]{2,1,0:T(8,128)(2,1)}, u32[]{:S(2)}, u32[]{:S(2)}) %all-to-all-start.1) | async-done | bytes 3670048 | tf_op jit(solution)/shard_map/all_to_all | solution.py:114
  356.1 6.5 %all-to-all-start.4 = ((bf16[16,24,1024]{2,1,0:T(8,128)(2,1)}), bf16[16,24,1024]{2,1,0:T(8,128)(2,1)}, u32[]{:S(2)}, u32[]{:S(2)}) async-start(bf16[16,24,1024]{2,1,0:T(8,128)(2,1)} %broadcast_select_fusion.2), calls=%async_computation.4 | async-start | bytes 1572864 | tf_op jit(solution)/shard_map/all_to_all | solution.py:137
  402.9 5.6 all-to-all-start.15
  410.1 17.3 %all-to-all-done.15 = bf16[16,24,1024]{2,1,0:T(8,128)(2,1)} async-done(((bf16[16,24,1024]{2,1,0:T(8,128)(2,1)}), bf16[16,24,1024]{2,1,0:T(8,128)(2,1)}, u32[]{:S(2)}, u32[]{:S(2)}) %all-to-all-start.15) | async-done | bytes 786464 | tf_op jit(solution)/shard_map/all_to_all | solution.py:185
  435.3 16.3 %all-to-all-done.13 = bf16[16,64,384]{2,1,0:T(8,128)(2,1)} async-done(((bf16[16,64,384]{2,1,0:T(8,128)(2,1)}), bf16[16,64,384]{2,1,0:T(8,128)(2,1)}, u32[]{:S(2)}, u32[]{:S(2)}) %all-to-all-start.13) | async-done | bytes 786464 | tf_op jit(solution)/shard_map/all_to_all | solution.py:184
  459.9 15.7 %all-to-all-done.11 = bf16[16,64,384]{2,1,0:T(8,128)(2,1)S(1)} async-done(((bf16[16,64,384]{2,1,0:T(8,128)(2,1)}), bf16[16,64,384]{2,1,0:T(8,128)(2,1)S(1)}, u32[]{:S(2)}, u32[]{:S(2)}) %all-to-all-start.11) | async-done | bytes 786464 | tf_op jit(solution)/shard_map/all_to_all | solution.py:183
  483.6 16.2 %all-to-all-done.16 = bf16[16,24,1024]{2,1,0:T(8,128)(2,1)} async-done(((bf16[16,24,1024]{2,1,0:T(8,128)(2,1)}), bf16[16,24,1024]{2,1,0:T(8,128)(2,1)}, u32[]{:S(2)}, u32[]{:S(2)}) %all-to-all-start.16) | async-done | bytes 786464 | tf_op jit(solution)/shard_map/all_to_all | solution.py:202
  506.7 17.3 %all-to-all-done.14 = bf16[16,64,384]{2,1,0:T(8,128)(2,1)} async-done(((bf16[16,64,384]{2,1,0:T(8,128)(2,1)}), bf16[16,64,384]{2,1,0:T(8,128)(2,1)}, u32[]{:S(2)}, u32[]{:S(2)}) %all-to-all-start.14) | async-done | bytes 786464 | tf_op jit(solution)/shard_map/all_to_all | solution.py:201
  537.9 10.2 %all-to-all-done.12 = bf16[16,64,384]{2,1,0:T(8,128)(2,1)S(1)} async-done(((bf16[16,64,384]{2,1,0:T(8,128)(2,1)}), bf16[16,64,384]{2,1,0:T(8,128)(2,1)S(1)}, u32[]{:S(2)}, u32[]{:S(2)}) %all-to-all-start.12) | async-done | bytes 786464 | tf_op jit(solution)/shard_map/all_to_all | solution.py:200
  554.9 6.8 %gather_fusion.3 = bf16[1024]{0:T(1024)(128)(2,1)S(1)} fusion(bf16[1792]{0:T(1024)(128)(2,1)S(1)} %reshape.489, s32[1024]{0:T(1024)S(1)} %broadcast_clamp_fusion), kind=kCustom, calls=%fused_computation.9 | custom fusion | bytes 8192 | tf_op jit(solution)/shard_map/jit(_take)/gather | solution.py:222
  573.5 60.3 %all-to-all-done.9 = bf16[16,112,1024]{2,1,0:T(8,128)(2,1)} async-done(((bf16[16,112,1024]{2,1,0:T(8,128)(2,1)}), bf16[16,112,1024]{2,1,0:T(8,128)(2,1)}, u32[]{:S(2)}, u32[]{:S(2)}) %all-to-all-start.9) | async-done | bytes 3670048 | tf_op jit(solution)/shard_map/all_to_all | solution.py:181
  633.8 7.5 %gather_fusion.2 = bf16[1024,1024]{1,0:T(8,128)(2,1)S(1)} fusion(bf16[1792,1024]{1,0:T(8,128)(2,1)} %bitcast.47, s32[1024]{0:T(1024)S(1)} %broadcast_clamp_fusion), kind=kCustom, calls=%fused_computation.8 | custom fusion | bytes 4198400 | tf_op jit(solution)/shard_map/jit(_take)/gather | solution.py:217
  (174 shorter events, 156.5 us)
Async XLA Ops:
  0.6 164.6 %copy-start = (bf16[128,1024]{1,0:T(8,128)(2,1)S(1)}, bf16[128,1024]{1,0:T(8,128)(2,1)}, u32[]{:S(2)}) copy-start(bf16[128,1024]{1,0:T(8,128)(2,1)} %param.14) | copy-start | bytes 786436
  19.8 21.0 %copy-start.2 = (bf16[128,8]{0,1:T(8,128)(2,1)S(1)}, bf16[128,8]{0,1:T(8,128)(2,1)}, u32[]{:S(2)}) copy-start(bf16[128,8]{0,1:T(8,128)(2,1)} %param.16) | copy-start | bytes 6148
  40.7 24.6 %copy-start.7 = (bf16[1,1024,384]{2,1,0:T(8,128)(2,1)S(1)}, bf16[1,1024,384]{2,1,0:T(8,128)(2,1)}, u32[]{:S(2)}) copy-start(bf16[1,1024,384]{2,1,0:T(8,128)(2,1)} %param.20) | copy-start | bytes 2359300
  40.8 48.2 %copy-start.4 = (bf16[1,1024,384]{2,1,0:T(8,128)(2,1)S(1)}, bf16[1,1024,384]{2,1,0:T(8,128)(2,1)}, u32[]{:S(2)}) copy-start(bf16[1,1024,384]{2,1,0:T(8,128)(2,1)} %param.19) | copy-start | bytes 2359300
  65.4 52.0 %copy-start.22 = (s32[16]{0:T(128)S(1)}, s32[16]{0:T(128)}, u32[]{:S(2)}) copy-start(s32[16]{0:T(128)} %param.18) | copy-start | bytes 196
  112.7 23.4 %all-to-all-start.3 = ((bf16[16,24,1024]{2,1,0:T(8,128)(2,1)}), bf16[16,24,1024]{2,1,0:T(8,128)(2,1)S(1)}, u32[]{:S(2)}, u32[]{:S(2)}) async-start(bf16[16,24,1024]{2,1,0:T(8,128)(2,1)} %bitcast.173), calls=%async_computation.3 | async-start | bytes 1572864 | tf_op jit(solution)/shard_map/all_to_all | solution.py:120
  160.6 23.7 %all-to-all-start.8 = ((bf16[16,64,384]{2,1,0:T(8,128)(2,1)}), bf16[16,64,384]{2,1,0:T(8,128)(2,1)S(1)}, u32[]{:S(2)}, u32[]{:S(2)}) async-start(bf16[16,64,384]{2,1,0:T(8,128)(2,1)} %get-tuple-element.56), calls=%async_computation.8 | async-start | bytes 1572864 | tf_op jit(solution)/shard_map/all_to_all | solution.py:123
  165.3 6.7 %copy-start.3 = (bf16[128,1024]{1,0:T(8,128)(2,1)S(1)}, bf16[128,1024]{1,0:T(8,128)(2,1)}, u32[]{:S(2)}) copy-start(bf16[128,1024]{1,0:T(8,128)(2,1)} %param.15) | copy-start | bytes 786436
  271.4 84.8 %all-to-all-start.1 = ((bf16[16,112,1024]{2,1,0:T(8,128)(2,1)}), bf16[16,112,1024]{2,1,0:T(8,128)(2,1)}, u32[]{:S(2)}, u32[]{:S(2)}) async-start(bf16[16,112,1024]{2,1,0:T(8,128)(2,1)} %bitcast.151), calls=%async_computation.1 | async-start | bytes 7340032 | tf_op jit(solution)/shard_map/all_to_all | solution.py:114
  356.1 25.4 %all-to-all-start.4 = ((bf16[16,24,1024]{2,1,0:T(8,128)(2,1)}), bf16[16,24,1024]{2,1,0:T(8,128)(2,1)}, u32[]{:S(2)}, u32[]{:S(2)}) async-start(bf16[16,24,1024]{2,1,0:T(8,128)(2,1)} %broadcast_select_fusion.2), calls=%async_computation.4 | async-start | bytes 1572864 | tf_op jit(solution)/shard_map/all_to_all | solution.py:137
  366.0 8.7 %copy-start.11 = (bf16[16,80,1024]{2,1,0:T(8,128)(2,1)}, bf16[16,80,1024]{2,1,0:T(8,128)(2,1)S(1)}, u32[]{:S(2)}) copy-start(bf16[16,80,1024]{2,1,0:T(8,128)(2,1)S(1)} %slice.88) | copy-start | bytes 7864324
  387.5 4.2 copy-start.13
  392.7 10.2 %all-to-all-start.10 = ((bf16[16,1,112]{2,1,0:T(2,128)(2,1)}), bf16[16,1,112]{2,1,0:T(2,128)(2,1)S(1)}, u32[]{:S(2)}, u32[]{:S(2)}) async-start(bf16[16,1,112]{2,1,0:T(2,128)(2,1)} %copy.158), calls=%async_computation.10 | async-start | bytes 16384 | tf_op jit(solution)/shard_map/all_to_all | solution.py:182
  402.9 24.5 %all-to-all-start.15 = ((bf16[16,24,1024]{2,1,0:T(8,128)(2,1)}), bf16[16,24,1024]{2,1,0:T(8,128)(2,1)}, u32[]{:S(2)}, u32[]{:S(2)}) async-start(bf16[16,24,1024]{2,1,0:T(8,128)(2,1)} %bitcast.175), calls=%async_computation.15 | async-start | bytes 1572864 | tf_op jit(solution)/shard_map/all_to_all | solution.py:185
  427.4 24.1 %all-to-all-start.13 = ((bf16[16,64,384]{2,1,0:T(8,128)(2,1)}), bf16[16,64,384]{2,1,0:T(8,128)(2,1)}, u32[]{:S(2)}, u32[]{:S(2)}) async-start(bf16[16,64,384]{2,1,0:T(8,128)(2,1)} %bitcast.177), calls=%async_computation.13 | async-start | bytes 1572864 | tf_op jit(solution)/shard_map/all_to_all | solution.py:184
  451.6 24.1 %all-to-all-start.11 = ((bf16[16,64,384]{2,1,0:T(8,128)(2,1)}), bf16[16,64,384]{2,1,0:T(8,128)(2,1)S(1)}, u32[]{:S(2)}, u32[]{:S(2)}) async-start(bf16[16,64,384]{2,1,0:T(8,128)(2,1)} %bitcast.176), calls=%async_computation.11 | async-start | bytes 1572864 | tf_op jit(solution)/shard_map/all_to_all | solution.py:183
  475.6 24.2 %all-to-all-start.16 = ((bf16[16,24,1024]{2,1,0:T(8,128)(2,1)}), bf16[16,24,1024]{2,1,0:T(8,128)(2,1)}, u32[]{:S(2)}, u32[]{:S(2)}) async-start(bf16[16,24,1024]{2,1,0:T(8,128)(2,1)} %copy.165), calls=%async_computation.16 | async-start | bytes 1572864 | tf_op jit(solution)/shard_map/all_to_all | solution.py:202
  499.8 24.2 %all-to-all-start.14 = ((bf16[16,64,384]{2,1,0:T(8,128)(2,1)}), bf16[16,64,384]{2,1,0:T(8,128)(2,1)}, u32[]{:S(2)}, u32[]{:S(2)}) async-start(bf16[16,64,384]{2,1,0:T(8,128)(2,1)} %copy.163), calls=%async_computation.14 | async-start | bytes 1572864 | tf_op jit(solution)/shard_map/all_to_all | solution.py:201
  524.0 24.1 %all-to-all-start.12 = ((bf16[16,64,384]{2,1,0:T(8,128)(2,1)}), bf16[16,64,384]{2,1,0:T(8,128)(2,1)S(1)}, u32[]{:S(2)}, u32[]{:S(2)}) async-start(bf16[16,64,384]{2,1,0:T(8,128)(2,1)} %copy.161), calls=%async_computation.12 | async-start | bytes 1572864 | tf_op jit(solution)/shard_map/all_to_all | solution.py:200
  548.9 84.9 %all-to-all-start.9 = ((bf16[16,112,1024]{2,1,0:T(8,128)(2,1)}), bf16[16,112,1024]{2,1,0:T(8,128)(2,1)}, u32[]{:S(2)}, u32[]{:S(2)}) async-start(bf16[16,112,1024]{2,1,0:T(8,128)(2,1)} %pad_maximum_fusion), calls=%async_computation.9 | async-start | bytes 7340032 | tf_op jit(solution)/shard_map/all_to_all | solution.py:181
  554.2 7.7 %copy-start.21 = (s32[128,8]{0,1:T(8,128)S(1)}, s32[128,8]{0,1:T(8,128)}, u32[]{:S(2)}) copy-start(s32[128,8]{0,1:T(8,128)} %param.17) | copy-start | bytes 12292
  554.2 8.7 %copy-start.12 = (bf16[16,80,1024]{2,1,0:T(8,128)(2,1)S(1)}, bf16[16,80,1024]{2,1,0:T(8,128)(2,1)}, u32[]{:S(2)}) copy-start(bf16[16,80,1024]{2,1,0:T(8,128)(2,1)} %copy-done.11) | copy-start | bytes 7864324
  562.9 4.0 copy-start.16
  633.8 9.9 %copy-start.1 = (bf16[128,1024]{1,0:T(8,128)(2,1)S(1)}, bf16[128,1024]{1,0:T(8,128)(2,1)}, u32[]{:S(2)}) copy-start(bf16[128,1024]{1,0:T(8,128)(2,1)} %param.14) | copy-start | bytes 786436
  (15 other events, 34.0 us)
where the time goes:
time: 648 us; the launch traced here: 644 us
  waiting for transfers between devices  248 us (38%)
  blocking collectives  170 us (26%)
  local copies, waits for them, and re-layouts  75.5 us (12%)
  starting transfers between devices  63.2 us (10%)
  other arithmetic  43.6 us (7%)
  matrix products  41.9 us (6%)
    all_to_all x1, blocking collectives, on_device(): lax.all_to_all(send_x, 'expert', split_axis=0, concat_axis=0, tiled=True)  87 us
    all_to_all x1, waiting for transfers between devices, on_device(): lax.all_to_all(send_dy, 'expert', split_axis=0, concat_axis=0, tiled=True)  75.8 us
    all_to_all x1, waiting for transfers between devices, on_device(): lax.all_to_all(back_x, 'expert', split_axis=0, concat_axis=0, tiled=True)  60.3 us
    all_to_all x1, blocking collectives, on_device(): lax.all_to_all(jnp.take(spread_up, replica_table, axis=0), 'expert', spli...  24.5 us
    all_to_all x1, blocking collectives, on_device(): lax.all_to_all(piece_gate, 'expert', split_axis=0, concat_axis=0, tiled=T...  23.8 us
    all_to_all x1, blocking collectives, on_device(): lax.all_to_all(piece_up, 'expert', split_axis=0, concat_axis=0, tiled=True)  23.6 us
    all_to_all x1, waiting for transfers between devices, on_device(): lax.all_to_all(replica_down, 'expert', split_axis=0, concat_axis=0, tiled...  17.3 us
    all_to_all x1, waiting for transfers between devices, on_device(): lax.all_to_all(summed_up, 'expert', split_axis=0, concat_axis=0, tiled=True)  17.3 us
  transfers between devices with their start and end apart: 12, of which 11 were waited for; matrix products, arithmetic and copies ran while one was open for 13% of the time, Pallas kernels for 0%

commit v1 on v0

v1 whole, which is shorter than its diff:
```python
import jax
import jax.numpy as jnp
from jax import lax
from jax.sharding import PartitionSpec as P

TOP = 8
ROWS_PER_CHUNK = 4096

contract_rows = (((0,), (0,)), ((), ()))
contract_cols = (((1,), (1,)), ((), ()))


def keep_plan(gates, row_ids, replica_table, source, devices, home_cap, rep_cap):
    tok = row_ids.shape[0]
    experts = jnp.arange(devices, dtype=jnp.int32)
    hot = row_ids[:, :, None] == experts[None, None, :]
    named = jnp.any(hot, axis=1)
    dense_gate = jnp.sum(jnp.where(hot, gates.astype(jnp.float32)[:, :, None], 0.0), axis=1)
    copies = 1 + jnp.sum((replica_table[:, None] == experts[None, :]).astype(jnp.int32), axis=0)
    order = jnp.arange(tok, dtype=jnp.int32)
    earlier = (order[:, None] > order[None, :]).astype(jnp.bfloat16)
    rank = jnp.dot(earlier, named.astype(jnp.bfloat16), preferred_element_type=jnp.float32)
    many = copies.astype(jnp.float32)[None, :]
    position = jnp.floor((rank + 0.5) / many)
    turn = rank + source.astype(jnp.float32)
    copy_index = turn - many * jnp.floor((turn + 0.5) / many)
    limit = jnp.where(copy_index < 0.5, float(home_cap), float(rep_cap))
    kept = named & (position < limit)
    return jnp.where(kept, dense_gate, 0.0).astype(jnp.bfloat16)


def expert_grads(x, dy, gate, gate_w, up_w, down_w):
    a = jnp.dot(x, gate_w, preferred_element_type=jnp.float32)
    b = jnp.dot(x, up_w, preferred_element_type=jnp.float32)
    u = lax.dot_general(dy, down_w, contract_cols, preferred_element_type=jnp.float32)
    sig = jax.nn.sigmoid(a)
    act = a * sig
    product = act * b
    hidden = product.astype(jnp.bfloat16).astype(jnp.float32)
    gate_grad = jnp.sum(hidden * u, axis=1, keepdims=True)
    gate_grad = jnp.where(gate > 0, gate_grad, 0.0)
    hg = (gate * product).astype(jnp.bfloat16)
    gu = gate * u
    da = (gu * b * sig * (1.0 + a * (1.0 - sig))).astype(jnp.bfloat16)
    db = (gu * act).astype(jnp.bfloat16)
    dx = lax.dot_general(da, gate_w, contract_cols, preferred_element_type=jnp.float32)
    dx = dx + lax.dot_general(db, up_w, contract_cols, preferred_element_type=jnp.float32)
    dwg = lax.dot_general(x, da, contract_rows, preferred_element_type=jnp.float32)
    dwu = lax.dot_general(x, db, contract_rows, preferred_element_type=jnp.float32)
    dwd = lax.dot_general(hg, dy, contract_rows, preferred_element_type=jnp.float32)
    return dx.astype(jnp.bfloat16), gate_grad, dwg, dwu, dwd


def on_device(tokens_in, grad_out, gates, expert_ids, replica_table, w_gate, w_up, w_down):
    devices = lax.axis_size("expert")
    me = lax.axis_index("expert")
    tok, width = tokens_in.shape
    home_cap = max(2, 5 * tok * TOP // (4 * devices))
    rep_cap = max(2, tok * TOP // (2 * devices))
    kept_gate = keep_plan(gates, expert_ids, replica_table, me, devices, home_cap, rep_cap)
    lanes = -(-devices // 128) * 128
    kept_gate = jnp.pad(kept_gate, ((0, 0), (0, lanes - devices)))
    payload = jnp.concatenate([tokens_in, grad_out, kept_gate], axis=1)
    chunks = max(1, devices * tok // ROWS_PER_CHUNK)
    part = tok // chunks
    mine = jnp.arange(lanes, dtype=jnp.int32)[None, :] == me
    backs, sums = [], None
    for c in range(chunks):
        rows = lax.all_gather(payload[c * part : (c + 1) * part], "expert", axis=0, tiled=True)
        gate = jnp.sum(
            jnp.where(mine, rows[:, 2 * width :].astype(jnp.float32), 0.0), axis=1, keepdims=True
        )
        dx, gate_grad, *grads = expert_grads(
            rows[:, :width], rows[:, width : 2 * width], gate, w_gate[0], w_up[0], w_down[0]
        )
        spread = jnp.where(mine, gate_grad, 0.0).astype(jnp.bfloat16)
        back = jnp.concatenate([dx, spread], axis=1)
        backs.append(lax.psum_scatter(back, "expert", scatter_dimension=0, tiled=True))
        sums = grads if sums is None else [p + q for p, q in zip(sums, grads)]
        if c + 1 < chunks:
            payload, sums = lax.optimization_barrier((payload, sums))
    back = jnp.concatenate(backs, axis=0)
    experts = jnp.arange(devices, dtype=jnp.int32)
    hot = expert_ids[:, :, None] == experts[None, None, :]
    picked = jnp.where(hot, back[:, None, width : width + devices].astype(jnp.float32), 0.0)
    grad_gates = jnp.sum(picked, axis=2).astype(jnp.bfloat16)
    return (back[:, :width], grad_gates, *[g.astype(jnp.bfloat16)[None] for g in sums])


def solution(mesh):
    return jax.shard_map(
        on_device,
        mesh=mesh,
        in_specs=(
            P(("groups", "expert"), None),
            P(("groups", "expert"), None),
            P(("groups", "expert"), None),
            P(("groups", "expert"), None),
            P("groups"),
            P("expert", None, None),
            P("expert", None, None),
            P("expert", None, None),
        ),
        out_specs=(
            P(("groups", "expert"), None),
            P(("groups", "expert"), None),
            P(("groups", "expert"), None, None),
            P(("groups", "expert"), None, None),
            P(("groups", "expert"), None, None),
        ),
        check_vma=False,
    )
```

time: 648 us -> 209 us (0.32)
  blocking collectives: 170 us -> 0 us
  waiting for transfers between devices: 248 us -> 138 us
  local copies, waits for them, and re-layouts: 75.5 us -> 12.2 us
  starting transfers between devices: 63.2 us -> 0.08 us
  other arithmetic: 43.6 us -> 8.25 us
  between operations: 1.17 us -> 14.2 us
  matrix products: 41.9 us -> 33.1 us
    all_to_all x12 -> x0, waiting for transfers between devices: 248 us -> none  [the longest x1 75.8 us: on_device(): lax.all_to_all(send_dy, 'expert', split_axis=0, concat_axis=0, tiled=True)]
    all_to_all x5 -> x0, blocking collectives: 170 us -> none  [the longest x1 87 us: on_device(): lax.all_to_all(send_x, 'expert', split_axis=0, concat_axis=0, tiled=True)]
    all_gather x0 -> x1, waiting for transfers between devices: none -> 80.2 us  [on_device(): lax.all_gather(payload[c * part:(c + 1) * part], 'expert', axis=0, tiled=...]
    all_to_all x12 -> x0, starting transfers between devices: 63.2 us -> none  [the longest x1 6.46 us: on_device(): lax.all_to_all(jnp.take(spread_down, replica_table, axis=0), 'expert', sp...]
    unnamed x0 -> x3, waiting for transfers between devices: none -> 58 us
    gather x15 -> x0, local copies, waits for them, and re-layouts: 52.1 us -> none  [the longest x1 13.4 us: on_device(): gates[token_row, top_index]]
    another operation x7 -> x0, other arithmetic: 14 us -> none
    select_n x8 -> x1, other arithmetic: 11.4 us -> 0.01 us  [expert_grads(): gate_grad = jnp.where(gate > 0, gate_grad, 0.0)]
  transfers between devices with their start and end apart: 12 -> 2, of which waited for: 11 -> 2; matrix products, arithmetic and copies ran while one was open for 13% -> 8% of each run, Pallas kernels for 0% -> 0%
where the time goes in v1:
time: 209 us; the launch traced here: 206 us
  waiting for transfers between devices  138 us (66%)
  matrix products  33.1 us (16%)
  between operations  14.2 us (7%)
  local copies, waits for them, and re-layouts  12.2 us (6%)
  other arithmetic  8.25 us (4%)
    all_gather x1, waiting for transfers between devices, on_device(): lax.all_gather(payload[c * part:(c + 1) * part], 'expert', axis=0, tiled=...  80.2 us
    unnamed x3, waiting for transfers between devices  58 us
    unnamed x22, local copies, waits for them, and re-layouts  9.72 us
    dot_general x1, matrix products, expert_grads(): lax.dot_general(x, da, contract_rows, preferred_element_type=jnp.float32)  5.91 us
    dot_general x1, matrix products, expert_grads(): lax.dot_general(x, db, contract_rows, preferred_element_type=jnp.float32)  5.78 us
    dot_general x1, matrix products, expert_grads(): lax.dot_general(hg, dy, contract_rows, preferred_element_type=jnp.float32)  5.54 us
    dot_general x1, matrix products, expert_grads(): a = jnp.dot(x, gate_w, preferred_element_type=jnp.float32)  4.98 us
    dot_general x1, matrix products, expert_grads(): b = jnp.dot(x, up_w, preferred_element_type=jnp.float32)  4.22 us
  transfers between devices with their start and end apart: 2, of which 2 were waited for; matrix products, arithmetic and copies ran while one was open for 8% of the time, Pallas kernels for 0%

profile of v1, /device:TPU:10, one launch (start us, length us, event | category | flops | bytes accessed | tf_op | source)
XLA Modules:
  0.0 206.0 jit_solution(4945060496822950731)
XLA Ops:
  7.2 0.8 convert_reduce_fusion
  8.1 0.7 fusion.41
  8.8 0.7 convert_element_type.66
  9.5 0.7 select_reduce_fusion.2
  10.2 1.1 copy.25
  11.3 1.1 copy.26
  12.6 0.8 fusion.40
  13.5 80.2 %all-gather.2.cloned.1.call-done = bf16[2048,2176]{0,1:T(8,128)(2,1)} async-done(((bf16[128,2176]{0,1:T(8,128)(2,1)}), bf16[2048,2176]{0,1:T(8,128)(2,1)}) %all-gather.2.cloned.1.call-update) | async-done | bytes 8912912 | tf_op jit(solution)/shard_map/all_gather | solution.py:69
  93.7 1.2 select_reduce_fusion
  95.0 4.2 %fusion.11 = f32[2048,384]{0,1:T(8,128)S(1)} fusion(bf16[2048,2176]{0,1:T(8,128)(2,1)} %all-gather.2.cloned.1.call-done, bf16[1,1024,384]{2,1,0:T(8,128)(2,1)S(1)} %copy-done.2), kind=kOutput, calls=%fused_computation.18 | convolution fusion | flops 1610612736 | bytes 8126464 | tf_op jit(solution)/shard_map/dot_general | solution.py:34
  99.2 0.5 copy-done.4
  99.9 1.8 fusion.2
  101.7 5.0 %multiply_convert_fusion.2 = (bf16[2048,384]{0,1:T(8,128)(2,1)S(1)}, bf16[2048]{0:T(1024)(128)(2,1)S(1)}, bf16[2048,384]{0,1:T(8,128)(2,1)S(1)}, f32[2048,384]{0,1:T(8,128)}) fusion(f32[2048,384]{0,1:T(8,128)S(1)} %fusion.11, f32[2048,384]{0,1:T(8,128)S(1)} %fusion.2, f32[2048]{0:T(1024)S(1)} %select_reduce_fusion, bf16[1,1024,384]{2,1,0:T(8,128)(2,1)S(1)} %copy-done, ...), kind=kOutput, calls=%fused_computation.9 | convolution fusion | flops 1625552896 | bytes 17575936 | tf_op jit(solution)/shard_map/dot_general | solution.py:33
  106.9 2.3 %fusion.34 = f32[2048,1024]{0,1:T(8,128)S(1)} fusion(bf16[2048,384]{0,1:T(8,128)(2,1)S(1)} %get-tuple-element.20, bf16[1,1024,384]{2,1,0:T(8,128)(2,1)S(1)} %copy-done), kind=kOutput, calls=%fused_computation.32 | convolution fusion | flops 1610612736 | bytes 10747904 | tf_op jit(solution)/shard_map/dot_general | solution.py:46
  109.2 2.4 %add_convert_fusion = bf16[2048,1024]{0,1:T(8,128)(2,1)S(1)} fusion(f32[2048,1024]{0,1:T(8,128)S(1)} %fusion.34, bf16[2048,384]{0,1:T(8,128)(2,1)S(1)} %get-tuple-element.22, bf16[1,1024,384]{2,1,0:T(8,128)(2,1)S(1)} %copy-done.2), kind=kOutput, calls=%fused_computation | convolution fusion | flops 1614807040 | bytes 14942208 | tf_op jit(solution)/shard_map/dot_general | solution.py:47
  111.6 2.5 %pad_maximum_fusion = bf16[2048,1152]{0,1:T(8,128)(2,1)} fusion(bf16[2048,128]{0,1:T(8,128)(2,1)S(1)} %select_convert_fusion, bf16[2048,1024]{0,1:T(8,128)(2,1)S(1)} %add_convert_fusion), kind=kLoop, calls=%fused_computation.1 | loop fusion | flops 9437184 | bytes 9437184 | tf_op jit(solution)/shard_map/concatenate | solution.py:77
  114.1 6.7 %copy.28 = bf16[2048,1152]{1,0:T(8,128)(2,1)} copy(bf16[2048,1152]{0,1:T(8,128)(2,1)} %pad_maximum_fusion) | data formatting | bytes 9437184
  120.8 5.9 %fusion.30 = bf16[1,1024,384]{2,1,0:T(8,128)(2,1)} fusion(bf16[2048,384]{0,1:T(8,128)(2,1)} %copy-done.1, bf16[2048,2176]{0,1:T(8,128)(2,1)} %all-gather.2.cloned.1.call-done), kind=kOutput, calls=%fused_computation.27 | convolution fusion | flops 1611005952 | bytes 6553600 | tf_op jit(solution)/shard_map/dot_general | solution.py:48
  126.7 5.8 %fusion.27 = bf16[1,1024,384]{2,1,0:T(8,128)(2,1)} fusion(bf16[2048,384]{0,1:T(8,128)(2,1)S(1)} %get-tuple-element.22, bf16[2048,2176]{0,1:T(8,128)(2,1)} %all-gather.2.cloned.1.call-done), kind=kOutput, calls=%fused_computation.26 | convolution fusion | flops 1611005952 | bytes 6553600 | tf_op jit(solution)/shard_map/dot_general | solution.py:49
  132.5 5.5 %fusion.24 = bf16[1,384,1024]{2,1,0:T(8,128)(2,1)} fusion(bf16[2048,2176]{0,1:T(8,128)(2,1)} %all-gather.2.cloned.1.call-done, f32[2048]{0:T(1024)S(1)} %select_reduce_fusion, f32[2048,384]{0,1:T(8,128)S(1)} %copy-done.7, f32[2048,384]{0,1:T(8,128)S(1)} %copy-done.8), kind=kOutput, calls=%fused_computation.25 | convolution fusion | flops 1616510976 | bytes 11280384 | tf_op jit(solution)/shard_map/dot_general | solution.py:50
  138.0 58.0 %reduce-scatter.4.cloned.1.call-done = bf16[128,1152]{1,0:T(8,128)(2,1)} async-done(((bf16[2048,1152]{1,0:T(8,128)(2,1)}), bf16[128,1152]{1,0:T(8,128)(2,1)}) %reduce-scatter.4.cloned.1.call-update) | async-done | bytes 294928
  196.0 0.8 slice.24
  196.9 0.6 select_reduce_fusion.1
  197.5 1.7 slice.23
  (28 shorter events, 0.7 us)
Async XLA Ops:
  7.2 94.6 %copy-start = (bf16[1,1024,384]{2,1,0:T(8,128)(2,1)S(1)}, bf16[1,1024,384]{2,1,0:T(8,128)(2,1)}, u32[]{:S(2)}) copy-start(bf16[1,1024,384]{2,1,0:T(8,128)(2,1)} %param.13) | copy-start | bytes 2359300
  7.2 87.8 %copy-start.2 = (bf16[1,1024,384]{2,1,0:T(8,128)(2,1)S(1)}, bf16[1,1024,384]{2,1,0:T(8,128)(2,1)}, u32[]{:S(2)}) copy-start(bf16[1,1024,384]{2,1,0:T(8,128)(2,1)} %param.14) | copy-start | bytes 2359300
  7.2 86.5 %all-gather.2.cloned.1.call-start = ((), (), s32[]{:S(2)}) async-start(), calls=%async_computation.1 | async-start | bytes 9469952 | tf_op jit(solution)/shard_map/all_gather | solution.py:69
  13.5 182.6 %reduce-scatter.4.cloned.1.call-start = ((), (), s32[]{:S(2)}) async-start(), calls=%async_computation.2 | async-start | bytes 5013504
  95.0 4.8 %copy-start.4 = (bf16[2048,2176]{0,1:T(8,128)(2,1)S(1)}, bf16[2048,2176]{0,1:T(8,128)(2,1)}, u32[]{:S(2)}) copy-start(bf16[2048,2176]{0,1:T(8,128)(2,1)} %all-gather.2.cloned.1.call-done) | copy-start | bytes 26738692
  95.0 4.9 %copy-start.5 = (bf16[1,384,1024]{2,1,0:T(8,128)(2,1)S(1)}, bf16[1,384,1024]{2,1,0:T(8,128)(2,1)}, u32[]{:S(2)}) copy-start(bf16[1,384,1024]{2,1,0:T(8,128)(2,1)} %param.15) | copy-start | bytes 2359300
  99.9 1.8 copy-start.6
  106.7 2.5 %copy-start.1 = (bf16[2048,384]{0,1:T(8,128)(2,1)}, bf16[2048,384]{0,1:T(8,128)(2,1)S(1)}, u32[]{:S(2)}) copy-start(bf16[2048,384]{0,1:T(8,128)(2,1)S(1)} %get-tuple-element.20) | copy-start | bytes 4718596
  126.7 5.8 %copy-start.7 = (f32[2048,384]{0,1:T(8,128)S(1)}, f32[2048,384]{0,1:T(8,128)}, u32[]{:S(2)}) copy-start(f32[2048,384]{0,1:T(8,128)} %copy-done.6) | copy-start | bytes 9437188
  126.7 5.8 %copy-start.8 = (f32[2048,384]{0,1:T(8,128)S(1)}, f32[2048,384]{0,1:T(8,128)}, u32[]{:S(2)}) copy-start(f32[2048,384]{0,1:T(8,128)} %get-tuple-element.23) | copy-start | bytes 9437188
  132.5 64.4 %copy-start.3 = (s32[128,8]{0,1:T(8,128)S(1)}, s32[128,8]{0,1:T(8,128)}, u32[]{:S(2)}) copy-start(s32[128,8]{0,1:T(8,128)} %param.11) | copy-start | bytes 12292
Sparse Core Ops, SparseCore 0:
  13.6 80.0 all-gather.1
  120.9 75.0 reduce-scatter.3

commit v2 on v1

--- a/solution.py
+++ b/solution.py
@@ -1,6 +1,8 @@
 import jax
 import jax.numpy as jnp
 from jax import lax
+from jax.experimental import pallas as pl
+from jax.experimental.pallas import tpu as pltpu
 from jax.sharding import PartitionSpec as P
 
 TOP = 8
@@ -8,6 +10,275 @@
 
 contract_rows = (((0,), (0,)), ((), ()))
 contract_cols = (((1,), (1,)), ((), ()))
+
+MESH = pl.DeviceIdType.MESH
+VMEM_GRANT = 48 * 2**20
+
+
+def place(depth):
+    me = lax.axis_index("expert")
+    z, y, c = me // 4, (me // 2) % 2, me % 2
+    return me, z, y, c, depth - 1
+
+
+def index_of(z, y, c):
+    return (z * 2 + y) * 2 + c
+
+
+def greet(z, y, c, last):
+    sem = pltpu.get_barrier_semaphore()
+
+    def hello(peer):
+        pl.semaphore_signal(sem, inc=1, device_id={"expert": peer}, device_id_type=MESH)
+
+    hello(index_of(z, y, 1 - c))
+    hello(index_of(z, 1 - y, c))
+    pl.when(z > 0)(lambda: hello(index_of(z - 1, y, c)))
+    pl.when(z < last)(lambda: hello(index_of(z + 1, y, c)))
+    pl.semaphore_wait(sem, 2 + (z > 0).astype(jnp.int32) + (z < last).astype(jnp.int32))
+
+
+class Sender:
+    def __init__(self, sems):
+        self.sems, self.used, self.pending = sems, 0, []
+
+    def send(self, cond, make):
+        slot = self.used
+        self.used += 1
+        if cond is None:
+            make(self.sems.at[slot]).start()
+        else:
+            pl.when(cond)(lambda: make(self.sems.at[slot]).start())
+        self.pending.append((cond, make, slot))
+
+    def drain(self):
+        for cond, make, slot in self.pending:
+            if cond is None:
+                make(self.sems.at[slot]).wait_send()
+            else:
+                pl.when(cond)(lambda make=make, slot=slot: make(self.sems.at[slot]).wait_send())
+
+
+def remote(src, dst, recv_sem, peer):
+    return lambda send_sem: pltpu.make_async_remote_copy(
+        src_ref=src(), dst_ref=dst(), send_sem=send_sem, recv_sem=recv_sem(),
+        device_id={"expert": peer()}, device_id_type=MESH,
+    )
+
+
+def both(p, q):
+    return q if p is None else p & q
+
+
+def gather_kernel(depth, split, x_ref, buf, send_sems, recv_sems, local_sem):
+    me, z, y, c, last = place(depth)
+    tok = x_ref.shape[0]
+    rows = (pl.ds(0, split), pl.ds(split, tok - split))
+    local = pltpu.make_async_copy(x_ref, buf.at[me], local_sem)
+    local.start()
+    greet(z, y, c, last)
+    out = Sender(send_sems)
+
+    def push(cond, b, part, peer, own=False):
+        src = (lambda: x_ref.at[rows[part]]) if own else (lambda: buf.at[b(), rows[part]])
+        out.send(
+            cond,
+            remote(src, lambda: buf.at[b(), rows[part]], lambda: recv_sems.at[b(), part], peer),
+        )
+
+    def arrived(b, part):
+        pltpu.make_async_copy(
+            buf.at[b, rows[part]], buf.at[b, rows[part]], recv_sems.at[b, part]
+        ).wait()
+
+    up = lambda: index_of(z + 1, y, c)
+    down = lambda: index_of(z - 1, y, c)
+    over = lambda: index_of(z, 1 - y, c)
+    twin = lambda: index_of(z, y, 1 - c)
+    can_up, can_down = z < last, z > 0
+    mine = lambda: me
+    push(None, mine, 0, over, True)
+    push(can_up, mine, 1, up, True)
+    push(can_down, mine, 1, down, True)
+    push(can_up, mine, 0, up, True)
+    push(can_down, mine, 0, down, True)
+    push(None, mine, 1, over, True)
+    push(None, mine, 0, twin, True)
+    push(None, mine, 1, twin, True)
+    across = lambda: index_of(z, 1 - y, c)
+    arrived(across(), 0)
+    push(can_up, across, 0, up)
+    push(can_down, across, 0, down)
+    push(None, across, 0, twin)
+
+    def crossed(d):
+        sides = ((None, 0),) if d == 0 else ((z >= d, -d), (z + d <= last, d))
+        for cond, off in sides:
+            b = lambda off=off: index_of(z + off, 1 - y, c)
+            if cond is None:
+                arrived(b(), 1)
+            else:
+                pl.when(cond)(lambda: arrived(b(), 1))
+            push(cond, b, 1, twin)
+
+    for d in range(1, depth):
+        own = [
+            (z >= d, lambda d=d: index_of(z - d, y, c), can_up, up),
+            (z + d <= last, lambda d=d: index_of(z + d, y, c), can_down, down),
+        ]
+        far = [
+            (z >= d, lambda d=d: index_of(z - d, 1 - y, c), can_up, up),
+            (z + d <= last, lambda d=d: index_of(z + d, 1 - y, c), can_down, down),
+        ]
+        for part, group in ((1, own), (0, own), (0, far)):
+            for here, b, more, onward in group:
+                pl.when(here)(lambda: arrived(b(), part))
+                push(both(here, more), b, part, onward)
+                if part == 1:
+                    push(here, b, 1, over)
+                push(here, b, part, twin)
+        crossed(d - 1)
+    crossed(depth - 1)
+    for part in range(2):
+        for zz in range(depth):
+            for yy in range(2):
+                arrived(index_of(zz, yy, 1 - c), part)
+    out.drain()
+    local.wait()
+
+
+def gather_rows(x, devices, split):
+    depth = devices // 4
+    tok, wide = x.shape
+    return pl.pallas_call(
+        lambda *refs: gather_kernel(depth, split, *refs),
+        out_shape=jax.ShapeDtypeStruct((devices, tok, wide), x.dtype),
+        in_specs=[pl.BlockSpec(memory_space=pltpu.VMEM)],
+        out_specs=pl.BlockSpec(memory_space=pltpu.VMEM),
+        scratch_shapes=[
+            pltpu.SemaphoreType.DMA((16 * depth,)),
+            pltpu.SemaphoreType.DMA((devices, 2)),
+            pltpu.SemaphoreType.DMA,
+        ],
+        compiler_params=pltpu.CompilerParams(
+            collective_id=0, has_side_effects=True, vmem_limit_bytes=VMEM_GRANT
+        ),
+    )(x)
+
+
+def scatter_kernel(
+    depth, split, part_ref, out_ref, rc, acc0, acc1, accx, ry1, rz0, rz1, ry0,
+    send_sems, rc_sems, ry1_sems, rz0_sems, rz1_sems, ry0_sem,
+):
+    me, z, y, c, last = place(depth)
+    tok = out_ref.shape[0]
+    head, tail = pl.ds(0, split), pl.ds(split, tok - split)
+    greet(z, y, c, last)
+    out = Sender(send_sems)
+    f32 = jnp.float32
+    bf16 = jnp.bfloat16
+    up = lambda: index_of(z + 1, y, c)
+    down = lambda: index_of(z - 1, y, c)
+    over = lambda: index_of(z, 1 - y, c)
+    twin = lambda: index_of(z, y, 1 - c)
+
+    def landed(ref, sem):
+        pltpu.make_async_copy(ref, ref, sem).wait()
+
+    order = []
+    for k in range(depth // 2):
+        order += [depth - 1 - k, k]
+    if depth % 2:
+        order.append(depth // 2)
+    for zz in order:
+        for off in (1, 0):
+            yy = (y + off) % 2
+            out.send(
+                None,
+                remote(
+                    lambda zz=zz, yy=yy: part_ref.at[index_of(zz, yy, 1 - c)],
+                    lambda zz=zz, yy=yy: rc.at[zz, yy],
+                    lambda zz=zz, yy=yy: rc_sems.at[zz, yy],
+                    twin,
+                ),
+            )
+    for zz in order:
+        for off in (1, 0):
+            yy = (y + off) % 2
+            landed(rc.at[zz, yy], rc_sems.at[zz, yy])
+            b = index_of(zz, yy, c)
+            acc0[zz, yy] = (part_ref[b, head].astype(f32) + rc[zz, yy, head].astype(f32)).astype(bf16)
+            rest = (part_ref[b, tail].astype(f32) + rc[zz, yy, tail].astype(f32)).astype(bf16)
+            if off:
+                accx[zz] = rest
+                out.send(
+                    None,
+                    remote(
+                        lambda zz=zz: accx.at[zz], lambda zz=zz: ry1.at[zz],
+                        lambda zz=zz: ry1_sems.at[zz], over,
+                    ),
+                )
+            else:
+                acc1[zz] = rest
+
+    def add_chain(way, zz):
+        landed(rz1.at[way, zz], rz1_sems.at[way, zz])
+        acc1[zz] = (acc1[zz].astype(f32) + rz1[way, zz].astype(f32)).astype(bf16)
+        landed(rz0.at[way, zz], rz0_sems.at[way, zz])
+        acc0[zz] = (acc0[zz].astype(f32) + rz0[way, zz].astype(f32)).astype(bf16)
+
+    for zz in order:
+        landed(ry1.at[zz], ry1_sems.at[zz])
+        acc1[zz] = (acc1[zz].astype(f32) + ry1[zz].astype(f32)).astype(bf16)
+        for way, going, has, peer in ((0, z < zz, z > 0, up), (1, z > zz, z < last, down)):
+            pl.when(both(going, has))(lambda: add_chain(way, zz))
+            out.send(
+                going,
+                remote(
+                    lambda zz=zz: acc1.at[zz], lambda way=way, zz=zz: rz1.at[way, zz],
+                    lambda way=way, zz=zz: rz1_sems.at[way, zz], peer,
+                ),
+            )
+            out.send(
+                going,
+                remote(
+                    lambda zz=zz: acc0.at[zz], lambda way=way, zz=zz: rz0.at[way, zz],
+                    lambda way=way, zz=zz: rz0_sems.at[way, zz], peer,
+                ),
+            )
+    pl.when(z > 0)(lambda: add_chain(0, z))
+    pl.when(z < last)(lambda: add_chain(1, z))
+    out.send(
+        None,
+        remote(lambda: acc0.at[z, 1 - y], lambda: ry0, lambda: ry0_sem, over),
+    )
+    out_ref[tail] = acc1[z]
+    landed(ry0, ry0_sem)
+    out_ref[head] = (acc0[z, y].astype(f32) + ry0[...].astype(f32)).astype(bf16)
+    out.drain()
+
+
+def scatter_rows(part, devices, split):
+    depth = devices // 4
+    _, tok, wide = part.shape
+    rest = tok - split
+    bf = lambda *shape: pltpu.VMEM(shape + (wide,), jnp.bfloat16)
+    dma = pltpu.SemaphoreType.DMA
+    return pl.pallas_call(
+        lambda *refs: scatter_kernel(depth, split, *refs),
+        out_shape=jax.ShapeDtypeStruct((tok, wide), part.dtype),
+        in_specs=[pl.BlockSpec(memory_space=pltpu.VMEM)],
+        out_specs=pl.BlockSpec(memory_space=pltpu.VMEM),
+        scratch_shapes=[
+            bf(depth, 2, tok), bf(depth, 2, split), bf(depth, rest), bf(depth, rest),
+            bf(depth, rest), bf(2, depth, 2, split), bf(2, depth, rest), bf(split),
+            dma((7 * depth + 2,)), dma((depth, 2)), dma((depth,)), dma((2, depth)),
+            dma((2, depth)), dma,
+        ],
+        compiler_params=pltpu.CompilerParams(
+            collective_id=1, has_side_effects=True, vmem_limit_bytes=VMEM_GRANT
+        ),
+    )(part)
 
 
 def keep_plan(gates, row_ids, replica_table, source, devices, home_cap, rep_cap):
@@ -63,10 +334,15 @@
     payload = jnp.concatenate([tokens_in, grad_out, kept_gate], axis=1)
     chunks = max(1, devices * tok // ROWS_PER_CHUNK)
     part = tok // chunks
+    relayed = chunks == 1 and devices % 4 == 0 and tok % 32 == 0
+    split = max(16, (3 * tok // 8) // 16 * 16)
     mine = jnp.arange(lanes, dtype=jnp.int32)[None, :] == me
     backs, sums = [], None
     for c in range(chunks):
-        rows = lax.all_gather(payload[c * part : (c + 1) * part], "expert", axis=0, tiled=True)
+        if relayed:
+            rows = gather_rows(payload, devices, split).reshape(devices * tok, -1)
+        else:
+            rows = lax.all_gather(payload[c * part : (c + 1) * part], "expert", axis=0, tiled=True)
         gate = jnp.sum(
             jnp.where(mine, rows[:, 2 * width :].astype(jnp.float32), 0.0), axis=1, keepdims=True
         )
@@ -75,7 +351,10 @@
         )
         spread = jnp.where(mine, gate_grad, 0.0).astype(jnp.bfloat16)
         back = jnp.concatenate([dx, spread], axis=1)
-        backs.append(lax.psum_scatter(back, "expert", scatter_dimension=0, tiled=True))
+        if relayed:
+            backs.append(scatter_rows(back.reshape(devices, tok, -1), devices, split))
+        else:
+            backs.append(lax.psum_scatter(back, "expert", scatter_dimension=0, tiled=True))
         sums = grads if sums is None else [p + q for p, q in zip(sums, grads)]
         if c + 1 < chunks:
             payload, sums = lax.optimization_barrier((payload, sums))

time: 209 us -> 159 us (0.76); the launches traced: 206 us -> 159 us
  waiting for transfers between devices: 138 us -> 0 us
  Pallas kernels: 0 us -> 114 us
  between operations: 14.2 us -> 0.82 us
  matrix products: 33.1 us -> 24.8 us
    pallas_call x0 -> x2, Pallas kernels: none -> 114 us  [the longest x1 58.7 us: scatter_rows(): pl.pallas_call(lambda *refs: scatter_kernel(depth, split, *refs), out_sha...]
    all_gather x1 -> x0, waiting for transfers between devices: 80.2 us -> none  [on_device(): lax.all_gather(payload[c * part:(c + 1) * part], 'expert', axis=0, tiled=...]
    unnamed x3 -> x0, waiting for transfers between devices: 58 us -> none
    concatenate x0 -> x1, local copies, waits for them, and re-layouts: none -> 6.77 us  [on_device(): back = jnp.concatenate([dx, spread], axis=1)]
    unnamed x22 -> x17, local copies, waits for them, and re-layouts: 9.72 us -> 3.14 us
    dot_general x1, matrix products: 5.54 us -> 2.88 us  [expert_grads(): lax.dot_general(hg, dy, contract_rows, preferred_element_type=jnp.float32)]
    dot_general x1, matrix products: 5.91 us -> 3.25 us  [expert_grads(): lax.dot_general(x, da, contract_rows, preferred_element_type=jnp.float32)]
    dot_general x1, matrix products: 5.78 us -> 3.27 us  [expert_grads(): lax.dot_general(x, db, contract_rows, preferred_element_type=jnp.float32)]
  transfers between devices with their start and end apart: 2 -> 0, of which waited for: 2 -> 0; matrix products, arithmetic and copies ran while one was open for 8% -> 0% of each run, Pallas kernels for 0% -> 0%
where the time goes in v2:
time: 159 us
  Pallas kernels  114 us (72%)
  matrix products  24.8 us (16%)
  local copies, waits for them, and re-layouts  12 us (8%)
  other arithmetic  7.41 us (5%)
    pallas_call x1, Pallas kernels, scatter_rows(): pl.pallas_call(lambda *refs: scatter_kernel(depth, split, *refs), out_sha...  58.7 us
    pallas_call x1, Pallas kernels, gather_rows(): pl.pallas_call(lambda *refs: gather_kernel(depth, split, *refs), out_shap...  55.2 us
    concatenate x1, local copies, waits for them, and re-layouts, on_device(): back = jnp.concatenate([dx, spread], axis=1)  6.77 us
    dot_general x1, matrix products, expert_grads(): a = jnp.dot(x, gate_w, preferred_element_type=jnp.float32)  4.44 us
    dot_general x1, matrix products, expert_grads(): b = jnp.dot(x, up_w, preferred_element_type=jnp.float32)  4.24 us
    dot_general x1, matrix products, expert_grads(): lax.dot_general(x, db, contract_rows, preferred_element_type=jnp.float32)  3.27 us
    dot_general x1, matrix products, expert_grads(): lax.dot_general(x, da, contract_rows, preferred_element_type=jnp.float32)  3.25 us

profile of v2, /device:TPU:10, one launch (start us, length us, event | category | flops | bytes accessed | tf_op | source)
XLA Modules:
  0.0 159.0 jit_solution(5827074486192859980)
XLA Ops:
  0.7 0.8 convert_reduce_fusion
  1.5 0.7 fusion.41
  2.2 0.7 convert_element_type.66
  2.9 0.7 select_reduce_fusion.2
  4.0 1.1 fusion.40.refs_0_
  5.1 55.2 %shard_map.119 = bf16[16,128,2176]{2,1,0:T(8,128)(2,1)} custom-call(bf16[128,2176]{1,0:T(8,128)(2,1)S(1)} %fusion.40.refs_0_), custom_call_target="tpu_custom_call" | custom-call | tf_op jit(solution)/shard_map/pallas_call | solution.py:153
  60.3 1.1 slice.20
  61.4 0.2 copy.37
  61.6 0.2 select_reduce_fusion
  61.8 4.2 %fusion.11 = f32[2048,384]{0,1:T(8,128)S(1)} fusion(bf16[2048,2176]{1,0:T(8,128)(2,1)} %bitcast.30, bf16[1,1024,384]{2,1,0:T(8,128)(2,1)S(1)} %copy-done.2), kind=kOutput, calls=%fused_computation.18 | convolution fusion | flops 1610612736 | bytes 8126464 | tf_op jit(solution)/shard_map/dot_general | solution.py:305
  66.1 0.5 slice-done.1
  66.7 1.8 %fusion.2 = f32[2048,384]{0,1:T(8,128)S(1)} fusion(bf16[2048,2176]{1,0:T(8,128)(2,1)S(1)} %bitcast.33, bf16[1,384,1024]{2,1,0:T(8,128)(2,1)S(1)} %copy-done.4), kind=kOutput, calls=%fused_computation.4 | convolution fusion | flops 1610612736 | bytes 8126464 | tf_op jit(solution)/shard_map/dot_general | solution.py:306
  68.5 4.4 %multiply_convert_fusion.2 = (bf16[2048,384]{0,1:T(8,128)(2,1)S(1)}, bf16[2048]{0:T(1024)(128)(2,1)S(1)}, bf16[2048,384]{0,1:T(8,128)(2,1)S(1)}, f32[2048,384]{0,1:T(8,128)S(1)}) fusion(f32[2048,384]{0,1:T(8,128)S(1)} %fusion.11, f32[2048,384]{0,1:T(8,128)S(1)} %fusion.2, f32[2048]{0:T(1024)S(1)} %select_reduce_fusion, ...), kind=kOutput, calls=%fused_computation.9 | convolution fusion | flops 1625552896 | bytes 17575936 | tf_op jit(solution)/shard_map/dot_general | solution.py:304
  73.0 2.9 %fusion.24 = bf16[1,384,1024]{2,1,0:T(8,128)(2,1)} fusion(bf16[2048,2176]{1,0:T(8,128)(2,1)S(1)} %bitcast.35, f32[2048]{0:T(1024)S(1)} %select_reduce_fusion, f32[2048,384]{0,1:T(8,128)S(1)} %fusion.11, f32[2048,384]{0,1:T(8,128)S(1)} %get-tuple-element.8), kind=kOutput, calls=%fused_computation.25 | convolution fusion | flops 1616510976 | bytes 11280384 | tf_op jit(solution)/shard_map/dot_general | solution.py:321
  76.0 3.3 %fusion.30 = bf16[1,1024,384]{2,1,0:T(8,128)(2,1)} fusion(bf16[2048,384]{0,1:T(8,128)(2,1)S(1)} %get-tuple-element.5, bf16[2048,2176]{1,0:T(8,128)(2,1)S(1)} %bitcast.36), kind=kOutput, calls=%fused_computation.27 | convolution fusion | flops 1611005952 | bytes 6553600 | tf_op jit(solution)/shard_map/dot_general | solution.py:319
  79.2 3.3 %fusion.27 = bf16[1,1024,384]{2,1,0:T(8,128)(2,1)} fusion(bf16[2048,384]{0,1:T(8,128)(2,1)S(1)} %get-tuple-element.7, bf16[2048,2176]{1,0:T(8,128)(2,1)S(1)} %bitcast.37), kind=kOutput, calls=%fused_computation.26 | convolution fusion | flops 1611005952 | bytes 6553600 | tf_op jit(solution)/shard_map/dot_general | solution.py:320
  82.5 2.3 %fusion.34 = f32[2048,1024]{0,1:T(8,128)S(1)} fusion(bf16[2048,384]{0,1:T(8,128)(2,1)S(1)} %get-tuple-element.5, bf16[1,1024,384]{2,1,0:T(8,128)(2,1)S(1)} %copy-done), kind=kOutput, calls=%fused_computation.32 | convolution fusion | flops 1610612736 | bytes 10747904 | tf_op jit(solution)/shard_map/dot_general | solution.py:317
  84.8 2.4 %add_convert_fusion = bf16[2048,1024]{0,1:T(8,128)(2,1)S(1)} fusion(f32[2048,1024]{0,1:T(8,128)S(1)} %fusion.34, bf16[2048,384]{0,1:T(8,128)(2,1)S(1)} %get-tuple-element.7, bf16[1,1024,384]{2,1,0:T(8,128)(2,1)S(1)} %copy-done.2), kind=kOutput, calls=%fused_computation | convolution fusion | flops 1614807040 | bytes 14942208 | tf_op jit(solution)/shard_map/dot_general | solution.py:318
  87.2 2.5 %pad_maximum_fusion = bf16[2048,1152]{0,1:T(8,128)(2,1)} fusion(bf16[2048,128]{0,1:T(8,128)(2,1)S(1)} %select_convert_fusion, bf16[2048,1024]{0,1:T(8,128)(2,1)S(1)} %add_convert_fusion), kind=kLoop, calls=%fused_computation.1 | loop fusion | flops 9437184 | bytes 9437184 | tf_op jit(solution)/shard_map/concatenate | solution.py:353
  89.7 6.8 %copy.34 = bf16[2048,1152]{1,0:T(8,128)(2,1)} copy(bf16[2048,1152]{0,1:T(8,128)(2,1)} %pad_maximum_fusion) | data formatting | bytes 9437184 | tf_op jit(solution)/shard_map/concatenate | solution.py:353
  96.5 2.3 %copy-done.1 = bf16[2048,1152]{1,0:T(8,128)(2,1)S(1)} copy-done((bf16[2048,1152]{1,0:T(8,128)(2,1)S(1)}, bf16[2048,1152]{1,0:T(8,128)(2,1)}, u32[]{:S(2)}) %copy-start.1) | copy-done | bytes 4718616
  98.8 58.7 %shard_map.120 = bf16[128,1152]{1,0:T(8,128)(2,1)S(1)} custom-call(bf16[16,128,1152]{2,1,0:T(8,128)(2,1)S(1)} %bitcast.28), custom_call_target="tpu_custom_call" | custom-call | tf_op jit(solution)/shard_map/pallas_call | solution.py:267
  157.6 0.8 slice.18
  158.4 0.6 select_reduce_fusion.1
  (24 shorter events, 0.7 us)
Async XLA Ops:
  0.6 67.9 %copy-start = (bf16[1,1024,384]{2,1,0:T(8,128)(2,1)S(1)}, bf16[1,1024,384]{2,1,0:T(8,128)(2,1)}, u32[]{:S(2)}) copy-start(bf16[1,1024,384]{2,1,0:T(8,128)(2,1)} %param.13) | copy-start | bytes 2359300
  5.1 56.7 %copy-start.2 = (bf16[1,1024,384]{2,1,0:T(8,128)(2,1)S(1)}, bf16[1,1024,384]{2,1,0:T(8,128)(2,1)}, u32[]{:S(2)}) copy-start(bf16[1,1024,384]{2,1,0:T(8,128)(2,1)} %param.14) | copy-start | bytes 2359300
  61.6 4.5 %slice-start = ((s8[8912896]{0:T(1024)(128)(4,1)}), s8[4194304]{0:T(1024)(128)(4,1)S(1)}, s32[]{:S(2)}) async-start(s8[8912896]{0:T(1024)(128)(4,1)} %bitcast.31), calls=%async_computation | async-start | bytes 8388608
  61.8 4.8 %slice-start.1 = ((s8[8912896]{0:T(1024)(128)(4,1)}), s8[4194304]{0:T(1024)(128)(4,1)S(1)}, s32[]{:S(2)}) async-start(s8[8912896]{0:T(1024)(128)(4,1)} %bitcast.31), calls=%async_computation.1 | async-start | bytes 8388608
  61.8 4.8 %slice-start.2 = ((s8[8912896]{0:T(1024)(128)(4,1)}), s8[524288]{0:T(1024)(128)(4,1)S(1)}, s32[]{:S(2)}) async-start(s8[8912896]{0:T(1024)(128)(4,1)} %bitcast.31), calls=%async_computation.2 | async-start | bytes 1048576
  61.8 4.8 %copy-start.4 = (bf16[1,384,1024]{2,1,0:T(8,128)(2,1)S(1)}, bf16[1,384,1024]{2,1,0:T(8,128)(2,1)}, u32[]{:S(2)}) copy-start(bf16[1,384,1024]{2,1,0:T(8,128)(2,1)} %param.15) | copy-start | bytes 2359300
  96.5 2.3 %copy-start.1 = (bf16[2048,1152]{1,0:T(8,128)(2,1)S(1)}, bf16[2048,1152]{1,0:T(8,128)(2,1)}, u32[]{:S(2)}) copy-start(bf16[2048,1152]{1,0:T(8,128)(2,1)} %copy.34) | copy-start | bytes 14155780
  98.8 59.5 %copy-start.3 = (s32[128,8]{0,1:T(8,128)S(1)}, s32[128,8]{0,1:T(8,128)}, u32[]{:S(2)}) copy-start(s32[128,8]{0,1:T(8,128)} %param.11) | copy-start | bytes 12292

commit v3 on v2

--- a/solution.py
+++ b/solution.py
@@ -167,11 +167,13 @@
 
 
 def scatter_kernel(
-    depth, split, part_ref, out_ref, rc, acc0, acc1, accx, ry1, rz0, rz1, ry0,
+    depth, split, part_ref, gate_ref, out_ref, rc, acc0, acc1, accx, ry1, rz0, rz1, ry0,
     send_sems, rc_sems, ry1_sems, rz0_sems, rz1_sems, ry0_sem,
 ):
     me, z, y, c, last = place(depth)
-    tok = out_ref.shape[0]
+    tok, wide = out_ref.shape
+    main = part_ref.shape[2]
+    spans = ((part_ref, pl.ds(0, main)), (gate_ref, pl.ds(main, wide - main)))
     head, tail = pl.ds(0, split), pl.ds(split, tok - split)
     greet(z, y, c, last)
     out = Sender(send_sems)
@@ -193,24 +195,30 @@
     for zz in order:
         for off in (1, 0):
             yy = (y + off) % 2
-            out.send(
-                None,
-                remote(
-                    lambda zz=zz, yy=yy: part_ref.at[index_of(zz, yy, 1 - c)],
-                    lambda zz=zz, yy=yy: rc.at[zz, yy],
-                    lambda zz=zz, yy=yy: rc_sems.at[zz, yy],
-                    twin,
-                ),
-            )
+            for k, (src, span) in enumerate(spans):
+                out.send(
+                    None,
+                    remote(
+                        lambda zz=zz, yy=yy, src=src: src.at[index_of(zz, yy, 1 - c)],
+                        lambda zz=zz, yy=yy, span=span: rc.at[zz, yy, :, span],
+                        lambda zz=zz, yy=yy, k=k: rc_sems.at[zz, yy, k],
+                        twin,
+                    ),
+                )
     for zz in order:
         for off in (1, 0):
             yy = (y + off) % 2
-            landed(rc.at[zz, yy], rc_sems.at[zz, yy])
             b = index_of(zz, yy, c)
-            acc0[zz, yy] = (part_ref[b, head].astype(f32) + rc[zz, yy, head].astype(f32)).astype(bf16)
-            rest = (part_ref[b, tail].astype(f32) + rc[zz, yy, tail].astype(f32)).astype(bf16)
+            rest = accx if off else acc1
+            for k, (src, span) in enumerate(spans):
+                landed(rc.at[zz, yy, :, span], rc_sems.at[zz, yy, k])
+                acc0[zz, yy, :, span] = (
+                    src[b, head].astype(f32) + rc[zz, yy, head, span].astype(f32)
+                ).astype(bf16)
+                rest[zz, :, span] = (
+                    src[b, tail].astype(f32) + rc[zz, yy, tail, span].astype(f32)
+                ).astype(bf16)
             if off:
-                accx[zz] = rest
                 out.send(
                     None,
                     remote(
@@ -218,8 +226,6 @@
                         lambda zz=zz: ry1_sems.at[zz], over,
                     ),
                 )
-            else:
-                acc1[zz] = rest
 
     def add_chain(way, zz):
         landed(rz1.at[way, zz], rz1_sems.at[way, zz])
@@ -258,27 +264,27 @@
     out.drain()
 
 
-def scatter_rows(part, devices, split):
+def scatter_rows(part, gate, devices, split):
     depth = devices // 4
-    _, tok, wide = part.shape
+    tok, wide = part.shape[1], part.shape[2] + gate.shape[2]
     rest = tok - split
     bf = lambda *shape: pltpu.VMEM(shape + (wide,), jnp.bfloat16)
     dma = pltpu.SemaphoreType.DMA
     return pl.pallas_call(
         lambda *refs: scatter_kernel(depth, split, *refs),
         out_shape=jax.ShapeDtypeStruct((tok, wide), part.dtype),
-        in_specs=[pl.BlockSpec(memory_space=pltpu.VMEM)],
+        in_specs=[pl.BlockSpec(memory_space=pltpu.VMEM)] * 2,
         out_specs=pl.BlockSpec(memory_space=pltpu.VMEM),
         scratch_shapes=[
             bf(depth, 2, tok), bf(depth, 2, split), bf(depth, rest), bf(depth, rest),
             bf(depth, rest), bf(2, depth, 2, split), bf(2, depth, rest), bf(split),
-            dma((7 * depth + 2,)), dma((depth, 2)), dma((depth,)), dma((2, depth)),
+            dma((9 * depth + 2,)), dma((depth, 2, 2)), dma((depth,)), dma((2, depth)),
             dma((2, depth)), dma,
         ],
         compiler_params=pltpu.CompilerParams(
             collective_id=1, has_side_effects=True, vmem_limit_bytes=VMEM_GRANT
         ),
-    )(part)
+    )(part, gate)
 
 
 def keep_plan(gates, row_ids, replica_table, source, devices, home_cap, rep_cap):
@@ -335,7 +341,7 @@
     chunks = max(1, devices * tok // ROWS_PER_CHUNK)
     part = tok // chunks
     relayed = chunks == 1 and devices % 4 == 0 and tok % 32 == 0
-    split = max(16, (3 * tok // 8) // 16 * 16)
+    split = max(16, tok // 8 // 16 * 16)
     mine = jnp.arange(lanes, dtype=jnp.int32)[None, :] == me
     backs, sums = [], None
     for c in range(chunks):
@@ -350,10 +356,11 @@
             rows[:, :width], rows[:, width : 2 * width], gate, w_gate[0], w_up[0], w_down[0]
         )
         spread = jnp.where(mine, gate_grad, 0.0).astype(jnp.bfloat16)
-        back = jnp.concatenate([dx, spread], axis=1)
         if relayed:
-            backs.append(scatter_rows(back.reshape(devices, tok, -1), devices, split))
+            dx, spread = dx.reshape(devices, tok, width), spread.reshape(devices, tok, lanes)
+            backs.append(scatter_rows(dx, spread, devices, split))
         else:
+            back = jnp.concatenate([dx, spread], axis=1)
             backs.append(lax.psum_scatter(back, "expert", scatter_dimension=0, tiled=True))
         sums = grads if sums is None else [p + q for p, q in zip(sums, grads)]
         if c + 1 < chunks:

time: 159 us -> 141 us (0.89)
  local copies, waits for them, and re-layouts: 12 us -> 1.08 us
  Pallas kernels: 114 us -> 108 us
    concatenate x1 -> x0, local copies, waits for them, and re-layouts: 6.77 us -> none  [on_device(): back = jnp.concatenate([dx, spread], axis=1)]
    pallas_call x1, Pallas kernels: 58.7 us -> 55.5 us  [scatter_rows(): pl.pallas_call(lambda *refs: scatter_kernel(depth, split, *refs), out_sha...]
    unnamed x17 -> x14, local copies, waits for them, and re-layouts: 3.14 us -> 0.04 us
    pallas_call x1, Pallas kernels: 55.2 us -> 52.7 us  [gather_rows(): pl.pallas_call(lambda *refs: gather_kernel(depth, split, *refs), out_shap...]
    concatenate x1 -> x0, other arithmetic: 2.5 us -> none  [on_device(): back = jnp.concatenate([dx, spread], axis=1)]
    dot_general x1, matrix products: 4.24 us -> 1.9 us  [expert_grads(): b = jnp.dot(x, up_w, preferred_element_type=jnp.float32)]
where the time goes in v3:
time: 141 us; the launch traced here: 140 us
  Pallas kernels  108 us (77%)
  matrix products  23.8 us (17%)
  other arithmetic  6.34 us (4%)
    pallas_call x1, Pallas kernels, scatter_rows(): pl.pallas_call(lambda *refs: scatter_kernel(depth, split, *refs), out_sha...  55.5 us
    pallas_call x1, Pallas kernels, gather_rows(): pl.pallas_call(lambda *refs: gather_kernel(depth, split, *refs), out_shap...  52.7 us
    dot_general x1, matrix products, expert_grads(): a = jnp.dot(x, gate_w, preferred_element_type=jnp.float32)  4.23 us
    dot_general x1, matrix products, expert_grads(): lax.dot_general(dy, down_w, contract_cols, preferred_element_type=jnp.flo...  3.36 us
    dot_general x1, matrix products, expert_grads(): lax.dot_general(x, da, contract_rows, preferred_element_type=jnp.float32)  3.26 us
    dot_general x1, matrix products, expert_grads(): lax.dot_general(x, db, contract_rows, preferred_element_type=jnp.float32)  3.25 us

profile of v3, /device:TPU:10, one launch (start us, length us, event | category | flops | bytes accessed | tf_op | source)
XLA Modules:
  0.0 140.3 jit_solution(15781458725123655011)
XLA Ops:
  0.6 0.0 copy-start
  0.7 0.8 convert_reduce_fusion
  1.5 0.7 fusion.41
  2.2 0.7 convert_element_type.67
  2.9 0.7 select_reduce_fusion.2
  3.6 0.1 copy.27
  3.7 0.1 copy.28
  3.8 0.2 select_convert_fusion.1
  4.0 1.1 fusion.40.refs_0_
  5.1 52.7 %shard_map.119 = bf16[16,128,2176]{2,1,0:T(8,128)(2,1)} custom-call(bf16[128,2176]{1,0:T(8,128)(2,1)S(1)} %fusion.40.refs_0_), custom_call_target="tpu_custom_call" | custom-call | tf_op jit(solution)/shard_map/pallas_call | solution.py:153
  57.8 1.4 %select_reduce_fusion = f32[2048]{0:T(1024)S(1)} fusion(bf16[2048,2176]{1,0:T(8,128)(2,1)} %bitcast.31, pred[128]{0:T(512)(128)(4,1)S(1)} %iota_compare_fusion.11), kind=kLoop, calls=%fused_computation.30 | loop fusion | flops 784384 | bytes 532608 | tf_op jit(solution)/shard_map/reduce_sum | solution.py:352
  59.2 4.2 %fusion.9 = f32[2048,384]{0,1:T(8,128)S(1)} fusion(bf16[2048,2176]{1,0:T(8,128)(2,1)} %bitcast.32, bf16[1,1024,384]{2,1,0:T(8,128)(2,1)S(1)} %copy-done), kind=kOutput, calls=%fused_computation.15 | convolution fusion | flops 1610612736 | bytes 8126464 | tf_op jit(solution)/shard_map/dot_general | solution.py:310
  63.5 1.9 %fusion.11 = f32[2048,384]{0,1:T(8,128)S(1)} fusion(bf16[2048,2176]{1,0:T(8,128)(2,1)S(1)} %bitcast.35, bf16[1,1024,384]{2,1,0:T(8,128)(2,1)S(1)} %copy-done.1), kind=kOutput, calls=%fused_computation.17 | convolution fusion | flops 1610612736 | bytes 8126464 | tf_op jit(solution)/shard_map/dot_general | solution.py:311
  65.4 2.8 %fusion.24 = bf16[1,384,1024]{2,1,0:T(8,128)(2,1)} fusion(bf16[2048,2176]{1,0:T(8,128)(2,1)S(1)} %bitcast.36, f32[2048]{0:T(1024)S(1)} %select_reduce_fusion, f32[2048,384]{0,1:T(8,128)S(1)} %fusion.11, f32[2048,384]{0,1:T(8,128)S(1)} %fusion.9), kind=kOutput, calls=%fused_computation.24 | convolution fusion | flops 1616510976 | bytes 11280384 | tf_op jit(solution)/shard_map/dot_general | solution.py:327
  68.2 3.4 %multiply_reduce_fusion = (bf16[2048]{0:T(1024)(128)(2,1)S(1)}, bf16[2048,384]{0,1:T(8,128)(2,1)S(1)}, bf16[2048,384]{0,1:T(8,128)(2,1)S(1)}) fusion(f32[2048,384]{0,1:T(8,128)S(1)} %fusion.11, f32[2048,384]{0,1:T(8,128)S(1)} %fusion.9, f32[2048]{0:T(1024)S(1)} %select_reduce_fusion, bf16[1,384,1024]{2,1,0:T(8,128)(2,1)S(1)} %copy-done.3, ...), kind=kOutput, calls=%fused_computation.6 | convolution fusion | flops 1625552896 | bytes 14430208 | tf_op jit(solution)/shard_map/dot_general | solution.py:312
  71.6 0.3 select_convert_fusion.refs_1_
  71.9 3.3 %fusion.30 = bf16[1,1024,384]{2,1,0:T(8,128)(2,1)} fusion(bf16[2048,384]{0,1:T(8,128)(2,1)S(1)} %get-tuple-element.6, bf16[2048,2176]{1,0:T(8,128)(2,1)S(1)} %bitcast.38), kind=kOutput, calls=%fused_computation.26 | convolution fusion | flops 1611005952 | bytes 6553600 | tf_op jit(solution)/shard_map/dot_general | solution.py:325
  75.2 3.3 %fusion.27 = bf16[1,1024,384]{2,1,0:T(8,128)(2,1)} fusion(bf16[2048,384]{0,1:T(8,128)(2,1)S(1)} %get-tuple-element.7, bf16[2048,2176]{1,0:T(8,128)(2,1)S(1)} %bitcast.39), kind=kOutput, calls=%fused_computation.25 | convolution fusion | flops 1611005952 | bytes 6553600 | tf_op jit(solution)/shard_map/dot_general | solution.py:326
  78.5 2.4 %fusion.34 = f32[2048,1024]{1,0:T(8,128)S(1)} fusion(bf16[2048,384]{0,1:T(8,128)(2,1)S(1)} %get-tuple-element.6, bf16[1,1024,384]{2,1,0:T(8,128)(2,1)S(1)} %copy-done), kind=kOutput, calls=%fused_computation.31 | convolution fusion | flops 1610612736 | bytes 10747904 | tf_op jit(solution)/shard_map/dot_general | solution.py:323
  80.9 2.4 %add_convert_fusion = bf16[2048,1024]{1,0:T(8,128)(2,1)S(1)} fusion(f32[2048,1024]{1,0:T(8,128)S(1)} %fusion.34, bf16[2048,384]{0,1:T(8,128)(2,1)S(1)} %get-tuple-element.7, bf16[1,1024,384]{2,1,0:T(8,128)(2,1)S(1)} %copy-done.1), kind=kOutput, calls=%fused_computation | convolution fusion | flops 1614807040 | bytes 14942208 | tf_op jit(solution)/shard_map/dot_general | solution.py:324
  83.3 55.5 %shard_map.120 = bf16[128,1152]{1,0:T(8,128)(2,1)S(1)} custom-call(bf16[16,128,1024]{2,1,0:T(8,128)(2,1)S(1)} %bitcast.30, bf16[16,128,128]{2,1,0:T(8,128)(2,1)S(1)} %select_convert_fusion.refs_1_), custom_call_target="tpu_custom_call" | custom-call | tf_op jit(solution)/shard_map/pallas_call | solution.py:273
  138.9 0.1 copy.29
  138.9 0.8 slice.18
  139.7 0.6 select_reduce_fusion.1
  (18 shorter events, 0.1 us)
Async XLA Ops:
  0.6 58.6 %copy-start = (bf16[1,1024,384]{2,1,0:T(8,128)(2,1)S(1)}, bf16[1,1024,384]{2,1,0:T(8,128)(2,1)}, u32[]{:S(2)}) copy-start(bf16[1,1024,384]{2,1,0:T(8,128)(2,1)} %param.13) | copy-start | bytes 2359300
  57.8 5.7 %slice-start = ((s8[8912896]{0:T(1024)(128)(4,1)}), s8[4194304]{0:T(1024)(128)(4,1)S(1)}, s32[]{:S(2)}) async-start(s8[8912896]{0:T(1024)(128)(4,1)} %bitcast.33), calls=%async_computation | async-start | bytes 8388608
  59.2 4.3 %slice-start.1 = ((s8[8912896]{0:T(1024)(128)(4,1)}), s8[4194304]{0:T(1024)(128)(4,1)S(1)}, s32[]{:S(2)}) async-start(s8[8912896]{0:T(1024)(128)(4,1)} %bitcast.33), calls=%async_computation.1 | async-start | bytes 8388608
  59.2 4.3 %slice-start.2 = ((s8[8912896]{0:T(1024)(128)(4,1)}), s8[524288]{0:T(1024)(128)(4,1)S(1)}, s32[]{:S(2)}) async-start(s8[8912896]{0:T(1024)(128)(4,1)} %bitcast.33), calls=%async_computation.2 | async-start | bytes 1048576
  59.2 4.3 %copy-start.1 = (bf16[1,1024,384]{2,1,0:T(8,128)(2,1)S(1)}, bf16[1,1024,384]{2,1,0:T(8,128)(2,1)}, u32[]{:S(2)}) copy-start(bf16[1,1024,384]{2,1,0:T(8,128)(2,1)} %param.14) | copy-start | bytes 2359300
  65.4 2.8 %copy-start.3 = (bf16[1,384,1024]{2,1,0:T(8,128)(2,1)S(1)}, bf16[1,384,1024]{2,1,0:T(8,128)(2,1)}, u32[]{:S(2)}) copy-start(bf16[1,384,1024]{2,1,0:T(8,128)(2,1)} %param.15) | copy-start | bytes 2359300
  83.3 56.4 %copy-start.2 = (s32[128,8]{0,1:T(8,128)S(1)}, s32[128,8]{0,1:T(8,128)}, u32[]{:S(2)}) copy-start(s32[128,8]{0,1:T(8,128)} %param.11) | copy-start | bytes 12292

commit v4 on v3

--- a/solution.py
+++ b/solution.py
@@ -70,7 +70,10 @@
     return q if p is None else p & q
 
 
-def gather_kernel(depth, split, x_ref, buf, send_sems, recv_sems, local_sem):
+def gather_kernel(
+    depth, split, x_ref, wg_ref, wu_ref, wd_ref, buf, da_ref, db_ref, hg_ref, dx_ref, gg_ref,
+    send_sems, recv_sems, local_sem,
+):
     me, z, y, c, last = place(depth)
     tok = x_ref.shape[0]
     rows = (pl.ds(0, split), pl.ds(split, tok - split))
@@ -111,8 +114,46 @@
     push(can_down, across, 0, down)
     push(None, across, 0, twin)
 
+    def sides_at(d):
+        return ((None, 0),) if d == 0 else ((z >= d, -d), (z + d <= last, d))
+
+    width = dx_ref.shape[2]
+    f32 = jnp.float32
+    bf16 = jnp.bfloat16
+
+    def level(zz):
+        for part in range(2):
+            for yy in range(2):
+                arrived(index_of(zz, yy, 1 - c), part)
+
+        def pair(i, carry):
+            at = pl.ds(zz * 4 + 2 * i, 2)
+            x = buf[at, :, pl.ds(0, width)].reshape(2 * tok, width)
+            dy = buf[at, :, pl.ds(width, width)].reshape(2 * tok, width)
+            gates = buf[at, :, pl.ds(2 * width, buf.shape[2] - 2 * width)].reshape(2 * tok, -1)
+            mine = lax.broadcasted_iota(jnp.int32, gates.shape, 1) == me
+            gate = jnp.sum(jnp.where(mine, gates.astype(f32), 0.0), axis=1, keepdims=True)
+            gate_grad, hg, da, db, dx = row_grads(
+                x, dy, gate, wg_ref[...], wu_ref[...], wd_ref[...]
+            )
+            hg_ref[at] = hg.reshape(2, tok, -1)
+            da_ref[at] = da.reshape(2, tok, -1)
+            db_ref[at] = db.reshape(2, tok, -1)
+            dx_ref[at] = dx.astype(bf16).reshape(2, tok, width)
+            gg_ref[at] = jnp.where(mine, gate_grad, 0.0).astype(bf16).reshape(2, tok, -1)
+            return carry
+
+        lax.fori_loop(0, 2, pair, 0)
+
+    def levels(d):
+        for cond, off in sides_at(d):
+            if cond is None:
+                level(z)
+            else:
+                pl.when(cond)(lambda: level(z + off))
+
     def crossed(d):
-        sides = ((None, 0),) if d == 0 else ((z >= d, -d), (z + d <= last, d))
+        sides = sides_at(d)
         for cond, off in sides:
             b = lambda off=off: index_of(z + off, 1 - y, c)
             if cond is None:
@@ -138,23 +179,26 @@
                     push(here, b, 1, over)
                 push(here, b, part, twin)
         crossed(d - 1)
+        if d == 1:
+            local.wait()
+        levels(d - 1)
     crossed(depth - 1)
-    for part in range(2):
-        for zz in range(depth):
-            for yy in range(2):
-                arrived(index_of(zz, yy, 1 - c), part)
+    if depth == 1:
+        local.wait()
+    levels(depth - 1)
     out.drain()
-    local.wait()
-
-
-def gather_rows(x, devices, split):
+
+
+def gather_rows(x, gate_w, up_w, down_w, devices, split):
     depth = devices // 4
     tok, wide = x.shape
+    hidden, width = down_w.shape
+    sizes = (wide, hidden, hidden, hidden, width, wide - 2 * width)
     return pl.pallas_call(
         lambda *refs: gather_kernel(depth, split, *refs),
-        out_shape=jax.ShapeDtypeStruct((devices, tok, wide), x.dtype),
-        in_specs=[pl.BlockSpec(memory_space=pltpu.VMEM)],
-        out_specs=pl.BlockSpec(memory_space=pltpu.VMEM),
+        out_shape=[jax.ShapeDtypeStruct((devices, tok, n), x.dtype) for n in sizes],
+        in_specs=[pl.BlockSpec(memory_space=pltpu.VMEM)] * 4,
+        out_specs=[pl.BlockSpec(memory_space=pltpu.VMEM)] * 6,
         scratch_shapes=[
             pltpu.SemaphoreType.DMA((16 * depth,)),
             pltpu.SemaphoreType.DMA((devices, 2)),
@@ -163,7 +207,7 @@
         compiler_params=pltpu.CompilerParams(
             collective_id=0, has_side_effects=True, vmem_limit_bytes=VMEM_GRANT
         ),
-    )(x)
+    )(x, gate_w, up_w, down_w)
 
 
 def scatter_kernel(
@@ -306,7 +350,7 @@
     return jnp.where(kept, dense_gate, 0.0).astype(jnp.bfloat16)
 
 
-def expert_grads(x, dy, gate, gate_w, up_w, down_w):
+def row_grads(x, dy, gate, gate_w, up_w, down_w):
     a = jnp.dot(x, gate_w, preferred_element_type=jnp.float32)
     b = jnp.dot(x, up_w, preferred_element_type=jnp.float32)
     u = lax.dot_general(dy, down_w, contract_cols, preferred_element_type=jnp.float32)
@@ -322,10 +366,14 @@
     db = (gu * act).astype(jnp.bfloat16)
     dx = lax.dot_general(da, gate_w, contract_cols, preferred_element_type=jnp.float32)
     dx = dx + lax.dot_general(db, up_w, contract_cols, preferred_element_type=jnp.float32)
+    return gate_grad, hg, da, db, dx
+
+
+def weight_grads(x, dy, hg, da, db):
     dwg = lax.dot_general(x, da, contract_rows, preferred_element_type=jnp.float32)
     dwu = lax.dot_general(x, db, contract_rows, preferred_element_type=jnp.float32)
     dwd = lax.dot_general(hg, dy, contract_rows, preferred_element_type=jnp.float32)
-    return dx.astype(jnp.bfloat16), gate_grad, dwg, dwu, dwd
+    return dwg, dwu, dwd
 
 
 def on_device(tokens_in, grad_out, gates, expert_ids, replica_table, w_gate, w_up, w_down):
@@ -346,22 +394,25 @@
     backs, sums = [], None
     for c in range(chunks):
         if relayed:
-            rows = gather_rows(payload, devices, split).reshape(devices * tok, -1)
+            rows, da, db, hg, dx, spread = gather_rows(
+                payload, w_gate[0], w_up[0], w_down[0], devices, split
+            )
+            backs.append(scatter_rows(dx, spread, devices, split))
+            rows, da, db, hg = [v.reshape(devices * tok, -1) for v in (rows, da, db, hg)]
         else:
             rows = lax.all_gather(payload[c * part : (c + 1) * part], "expert", axis=0, tiled=True)
-        gate = jnp.sum(
-            jnp.where(mine, rows[:, 2 * width :].astype(jnp.float32), 0.0), axis=1, keepdims=True
-        )
-        dx, gate_grad, *grads = expert_grads(
-            rows[:, :width], rows[:, width : 2 * width], gate, w_gate[0], w_up[0], w_down[0]
-        )
-        spread = jnp.where(mine, gate_grad, 0.0).astype(jnp.bfloat16)
-        if relayed:
-            dx, spread = dx.reshape(devices, tok, width), spread.reshape(devices, tok, lanes)
-            backs.append(scatter_rows(dx, spread, devices, split))
-        else:
-            back = jnp.concatenate([dx, spread], axis=1)
+            gate = jnp.sum(
+                jnp.where(mine, rows[:, 2 * width :].astype(jnp.float32), 0.0),
+                axis=1,
+                keepdims=True,
+            )
+            gate_grad, hg, da, db, dx = row_grads(
+                rows[:, :width], rows[:, width : 2 * width], gate, w_gate[0], w_up[0], w_down[0]
+            )
+            spread = jnp.where(mine, gate_grad, 0.0).astype(jnp.bfloat16)
+            back = jnp.concatenate([dx.astype(jnp.bfloat16), spread], axis=1)
             backs.append(lax.psum_scatter(back, "expert", scatter_dimension=0, tiled=True))
+        grads = weight_grads(rows[:, :width], rows[:, width : 2 * width], hg, da, db)
         sums = grads if sums is None else [p + q for p, q in zip(sums, grads)]
         if c + 1 < chunks:
             payload, sums = lax.optimization_barrier((payload, sums))

time: 141 us -> 136 us (0.965)
  matrix products: 23.8 us -> 12.2 us
  Pallas kernels: 108 us -> 113 us
  local copies, waits for them, and re-layouts: 1.08 us -> 4.36 us
  other arithmetic: 6.34 us -> 4.64 us
    dot_general x8 -> x3, matrix products: 23.6 us -> 12 us  [the longest x1 6.08 us: weight_grads(): lax.dot_general(x, db, contract_rows, preferred_element_type=jnp.float32)]
    pallas_call x1, Pallas kernels: 52.7 us -> 56.8 us  [gather_rows(): pl.pallas_call(lambda *refs: gather_kernel(depth, split, *refs), out_shap...]
    unnamed x14, local copies, waits for them, and re-layouts: 0.04 us -> 3.33 us
where the time goes in v4:
time: 136 us; the launch traced here: 135 us
  Pallas kernels  113 us (83%)
  matrix products  12.2 us (9%)
  other arithmetic  4.64 us (3%)
  local copies, waits for them, and re-layouts  4.36 us (3%)
    pallas_call x1, Pallas kernels, gather_rows(): pl.pallas_call(lambda *refs: gather_kernel(depth, split, *refs), out_shap...  56.8 us
    pallas_call x1, Pallas kernels, scatter_rows(): pl.pallas_call(lambda *refs: scatter_kernel(depth, split, *refs), out_sha...  56.6 us
    dot_general x1, matrix products, weight_grads(): lax.dot_general(x, db, contract_rows, preferred_element_type=jnp.float32)  6.08 us
    unnamed x14, local copies, waits for them, and re-layouts  3.33 us
    dot_general x1, matrix products, weight_grads(): lax.dot_general(x, da, contract_rows, preferred_element_type=jnp.float32)  3.25 us

profile of v4, /device:TPU:10, one launch (start us, length us, event | category | flops | bytes accessed | tf_op | source)
XLA Modules:
  0.0 135.3 jit_solution(9234451378231862616)
XLA Ops:
  0.7 0.9 convert_reduce_fusion
  1.5 0.7 fusion.26
  2.2 0.7 convert_element_type.42
  2.9 0.7 select_reduce_fusion.1
  3.6 0.1 copy.27
  3.7 0.1 copy.28
  3.8 0.2 select_convert_fusion
  4.0 1.1 fusion.25.refs_0_
  5.1 0.0 copy-done.2
  5.1 0.0 copy-done.1
  5.1 0.0 copy-start.3
  5.1 1.1 copy-done.3
  6.3 56.8 %shard_map.119 = (bf16[16,128,2176]{2,1,0:T(8,128)(2,1)}, bf16[16,128,384]{2,1,0:T(8,128)(2,1)S(1)}, bf16[16,128,384]{2,1,0:T(8,128)(2,1)}, bf16[16,128,384]{2,1...) custom-call(bf16[128,2176]{1,0:T(8,128)(2,1)S(1)} %fusion.25.refs_0_, ...), custom_call_target="tpu_custom_call" | custom-call | tf_op jit(solution)/shard_map/pallas_call | solution.py:197
  63.1 0.0 copy-start
  63.1 2.2 %copy-done = bf16[16,128,1024]{2,1,0:T(8,128)(2,1)S(1)} copy-done((bf16[16,128,1024]{2,1,0:T(8,128)(2,1)S(1)}, bf16[16,128,1024]{2,1,0:T(8,128)(2,1)}, u32[]{:S(2)}) %copy-start) | copy-done | bytes 4194328
  65.3 56.6 %shard_map.120 = bf16[128,1152]{1,0:T(8,128)(2,1)S(1)} custom-call(bf16[16,128,1024]{2,1,0:T(8,128)(2,1)S(1)} %copy-done, bf16[16,128,128]{2,1,0:T(8,128)(2,1)S(1)} %get-tuple-element.12.refs_1_), custom_call_target="tpu_custom_call" | custom-call | tf_op jit(solution)/shard_map/pallas_call | solution.py:317
  121.9 0.1 copy.29
  121.9 0.8 slice.12
  122.7 0.0 copy-done.4
  122.7 0.6 select_reduce_fusion
  123.3 6.1 %fusion.18 = bf16[1,1024,384]{2,1,0:T(8,128)(2,1)} fusion(bf16[2048,384]{1,0:T(8,128)(2,1)} %bitcast.25, bf16[2048,2176]{1,0:T(8,128)(2,1)} %bitcast.21), kind=kOutput, calls=%fused_computation.10 | convolution fusion | flops 1611005952 | bytes 6553600 | tf_op jit(solution)/shard_map/dot_general | solution.py:374
  129.4 0.0 copy-done.5
  129.4 2.7 %fusion.15 = bf16[1,384,1024]{2,1,0:T(8,128)(2,1)} fusion(bf16[2048,384]{1,0:T(8,128)(2,1)S(1)} %bitcast.24, bf16[2048,2176]{1,0:T(8,128)(2,1)S(1)} %bitcast.22), kind=kOutput, calls=%fused_computation.9 | convolution fusion | flops 1611005952 | bytes 6553600 | tf_op jit(solution)/shard_map/dot_general | solution.py:375
  132.1 3.3 %fusion.21 = bf16[1,1024,384]{2,1,0:T(8,128)(2,1)} fusion(bf16[2048,384]{1,0:T(8,128)(2,1)S(1)} %bitcast.20, bf16[2048,2176]{1,0:T(8,128)(2,1)S(1)} %bitcast.23), kind=kOutput, calls=%fused_computation.11 | convolution fusion | flops 1611005952 | bytes 6553600 | tf_op jit(solution)/shard_map/dot_general | solution.py:373
  (8 shorter events, 0.0 us)
Async XLA Ops:
  0.6 4.5 %copy-start.2 = (bf16[1,1024,384]{2,1,0:T(8,128)(2,1)S(1)}, bf16[1,1024,384]{2,1,0:T(8,128)(2,1)}, u32[]{:S(2)}) copy-start(bf16[1,1024,384]{2,1,0:T(8,128)(2,1)} %param.14) | copy-start | bytes 2359300
  0.6 4.5 %copy-start.1 = (bf16[1,1024,384]{2,1,0:T(8,128)(2,1)S(1)}, bf16[1,1024,384]{2,1,0:T(8,128)(2,1)}, u32[]{:S(2)}) copy-start(bf16[1,1024,384]{2,1,0:T(8,128)(2,1)} %param.13) | copy-start | bytes 2359300
  5.1 1.1 copy-start.3
  63.1 2.2 %copy-start = (bf16[16,128,1024]{2,1,0:T(8,128)(2,1)S(1)}, bf16[16,128,1024]{2,1,0:T(8,128)(2,1)}, u32[]{:S(2)}) copy-start(bf16[16,128,1024]{2,1,0:T(8,128)(2,1)} %get-tuple-element.11.refs_0_) | copy-start | bytes 12582916
  65.2 57.5 %copy-start.4 = (s32[128,8]{0,1:T(8,128)S(1)}, s32[128,8]{0,1:T(8,128)}, u32[]{:S(2)}) copy-start(s32[128,8]{0,1:T(8,128)} %param.11) | copy-start | bytes 12292
  123.3 6.1 %copy-start.5 = (bf16[16,128,2176]{2,1,0:T(8,128)(2,1)S(1)}, bf16[16,128,2176]{2,1,0:T(8,128)(2,1)}, u32[]{:S(2)}) copy-start(bf16[16,128,2176]{2,1,0:T(8,128)(2,1)} %get-tuple-element.13) | copy-start | bytes 26738692
  123.3 6.1 %copy-start.6 = (bf16[16,128,384]{2,1,0:T(8,128)(2,1)S(1)}, bf16[16,128,384]{2,1,0:T(8,128)(2,1)}, u32[]{:S(2)}) copy-start(bf16[16,128,384]{2,1,0:T(8,128)(2,1)} %get-tuple-element.16) | copy-start | bytes 4718596

commit v5 on v4

--- a/solution.py
+++ b/solution.py
@@ -249,7 +249,7 @@
                         twin,
                     ),
                 )
-    for zz in order:
+    def fold(zz):
         for off in (1, 0):
             yy = (y + off) % 2
             b = index_of(zz, yy, c)
@@ -277,7 +277,7 @@
         landed(rz0.at[way, zz], rz0_sems.at[way, zz])
         acc0[zz] = (acc0[zz].astype(f32) + rz0[way, zz].astype(f32)).astype(bf16)
 
-    for zz in order:
+    def chain(zz):
         landed(ry1.at[zz], ry1_sems.at[zz])
         acc1[zz] = (acc1[zz].astype(f32) + ry1[zz].astype(f32)).astype(bf16)
         for way, going, has, peer in ((0, z < zz, z > 0, up), (1, z > zz, z < last, down)):
@@ -296,6 +296,11 @@
                     lambda way=way, zz=zz: rz0_sems.at[way, zz], peer,
                 ),
             )
+    fold(order[0])
+    for k in range(depth):
+        if k + 1 < depth:
+            fold(order[k + 1])
+        chain(order[k])
     pl.when(z > 0)(lambda: add_chain(0, z))
     pl.when(z < last)(lambda: add_chain(1, z))
     out.send(

time: 136 us -> 136 us (level)
  no operation moved by 1% of the time
where the time goes in v5:
time: 136 us; the launch traced here: 135 us
  Pallas kernels  113 us (83%)
  matrix products  12.2 us (9%)
  other arithmetic  4.64 us (3%)
  local copies, waits for them, and re-layouts  4.36 us (3%)
    pallas_call x1, Pallas kernels, gather_rows(): pl.pallas_call(lambda *refs: gather_kernel(depth, split, *refs), out_shap...  56.8 us
    pallas_call x1, Pallas kernels, scatter_rows(): pl.pallas_call(lambda *refs: scatter_kernel(depth, split, *refs), out_sha...  56.6 us
    dot_general x1, matrix products, weight_grads(): lax.dot_general(x, db, contract_rows, preferred_element_type=jnp.float32)  6.08 us
    unnamed x14, local copies, waits for them, and re-layouts  3.33 us
    dot_general x1, matrix products, weight_grads(): lax.dot_general(x, da, contract_rows, preferred_element_type=jnp.float32)  3.25 us

profile of v5, /device:TPU:10, one launch (start us, length us, event | category | flops | bytes accessed | tf_op | source)
XLA Modules:
  0.0 135.3 jit_solution(6677925339124030688)
XLA Ops:
  0.6 0.0 copy-start.2
  0.7 0.9 convert_reduce_fusion
  1.5 0.7 fusion.26
  2.2 0.7 convert_element_type.42
  2.9 0.7 select_reduce_fusion.1
  3.6 0.1 copy.27
  3.7 0.1 copy.28
  3.8 0.2 select_convert_fusion
  4.0 1.1 fusion.25.refs_0_
  5.1 0.0 copy-done.2
  5.1 0.0 copy-done.1
  5.1 0.0 copy-start.3
  5.1 1.1 copy-done.3
  6.3 56.8 %shard_map.119 = (bf16[16,128,2176]{2,1,0:T(8,128)(2,1)}, bf16[16,128,384]{2,1,0:T(8,128)(2,1)S(1)}, bf16[16,128,384]{2,1,0:T(8,128)(2,1)}, bf16[16,128,384]{2,1...) custom-call(bf16[128,2176]{1,0:T(8,128)(2,1)S(1)} %fusion.25.refs_0_, ...), custom_call_target="tpu_custom_call" | custom-call | tf_op jit(solution)/shard_map/pallas_call | solution.py:197
  63.1 0.0 copy-start
  63.1 2.2 %copy-done = bf16[16,128,1024]{2,1,0:T(8,128)(2,1)S(1)} copy-done((bf16[16,128,1024]{2,1,0:T(8,128)(2,1)S(1)}, bf16[16,128,1024]{2,1,0:T(8,128)(2,1)}, u32[]{:S(2)}) %copy-start) | copy-done | bytes 4194328
  65.3 56.6 %shard_map.120 = bf16[128,1152]{1,0:T(8,128)(2,1)S(1)} custom-call(bf16[16,128,1024]{2,1,0:T(8,128)(2,1)S(1)} %copy-done, bf16[16,128,128]{2,1,0:T(8,128)(2,1)S(1)} %get-tuple-element.12.refs_1_), custom_call_target="tpu_custom_call" | custom-call | tf_op jit(solution)/shard_map/pallas_call | solution.py:322
  121.9 0.1 copy.29
  122.0 0.8 slice.12
  122.7 0.6 select_reduce_fusion
  123.3 6.1 %fusion.18 = bf16[1,1024,384]{2,1,0:T(8,128)(2,1)} fusion(bf16[2048,384]{1,0:T(8,128)(2,1)} %bitcast.25, bf16[2048,2176]{1,0:T(8,128)(2,1)} %bitcast.21), kind=kOutput, calls=%fused_computation.10 | convolution fusion | flops 1611005952 | bytes 6553600 | tf_op jit(solution)/shard_map/dot_general | solution.py:379
  129.4 0.0 copy-done.5
  129.4 2.7 %fusion.15 = bf16[1,384,1024]{2,1,0:T(8,128)(2,1)} fusion(bf16[2048,384]{1,0:T(8,128)(2,1)S(1)} %bitcast.24, bf16[2048,2176]{1,0:T(8,128)(2,1)S(1)} %bitcast.22), kind=kOutput, calls=%fused_computation.9 | convolution fusion | flops 1611005952 | bytes 6553600 | tf_op jit(solution)/shard_map/dot_general | solution.py:380
  132.1 3.3 %fusion.21 = bf16[1,1024,384]{2,1,0:T(8,128)(2,1)} fusion(bf16[2048,384]{1,0:T(8,128)(2,1)S(1)} %bitcast.20, bf16[2048,2176]{1,0:T(8,128)(2,1)S(1)} %bitcast.23), kind=kOutput, calls=%fused_computation.11 | convolution fusion | flops 1611005952 | bytes 6553600 | tf_op jit(solution)/shard_map/dot_general | solution.py:378
  (8 shorter events, 0.0 us)
Async XLA Ops:
  0.6 4.5 %copy-start.2 = (bf16[1,1024,384]{2,1,0:T(8,128)(2,1)S(1)}, bf16[1,1024,384]{2,1,0:T(8,128)(2,1)}, u32[]{:S(2)}) copy-start(bf16[1,1024,384]{2,1,0:T(8,128)(2,1)} %param.14) | copy-start | bytes 2359300
  0.6 4.5 %copy-start.1 = (bf16[1,1024,384]{2,1,0:T(8,128)(2,1)S(1)}, bf16[1,1024,384]{2,1,0:T(8,128)(2,1)}, u32[]{:S(2)}) copy-start(bf16[1,1024,384]{2,1,0:T(8,128)(2,1)} %param.13) | copy-start | bytes 2359300
  5.1 1.1 copy-start.3
  63.1 2.2 %copy-start = (bf16[16,128,1024]{2,1,0:T(8,128)(2,1)S(1)}, bf16[16,128,1024]{2,1,0:T(8,128)(2,1)}, u32[]{:S(2)}) copy-start(bf16[16,128,1024]{2,1,0:T(8,128)(2,1)} %get-tuple-element.11.refs_0_) | copy-start | bytes 12582916
  65.2 57.5 %copy-start.4 = (s32[128,8]{0,1:T(8,128)S(1)}, s32[128,8]{0,1:T(8,128)}, u32[]{:S(2)}) copy-start(s32[128,8]{0,1:T(8,128)} %param.11) | copy-start | bytes 12292
  123.3 6.1 %copy-start.5 = (bf16[16,128,2176]{2,1,0:T(8,128)(2,1)S(1)}, bf16[16,128,2176]{2,1,0:T(8,128)(2,1)}, u32[]{:S(2)}) copy-start(bf16[16,128,2176]{2,1,0:T(8,128)(2,1)} %get-tuple-element.13) | copy-start | bytes 26738692
  123.3 6.1 %copy-start.6 = (bf16[16,128,384]{2,1,0:T(8,128)(2,1)S(1)}, bf16[16,128,384]{2,1,0:T(8,128)(2,1)}, u32[]{:S(2)}) copy-start(bf16[16,128,384]{2,1,0:T(8,128)(2,1)} %get-tuple-element.16) | copy-start | bytes 4718596
